TPU v7x, 512 devices: a whole 4x4x16 slice. The times are simulated.
512 devices in a mesh: len: 128 (over y, z, core), pipe: 4 (over x).
Axes of the slice: x: 4, y: 4, z: 16, core: 2. Of those that a mesh axis runs over, the one named last changes fastest.
Arguments:
- inputs: bfloat16 [512, 2048, 256], P(('len', 'pipe')), may hold values from -6 to 6
- cotangent: bfloat16 [512, 2048, 256], P(('len', 'pipe')), may hold values from -6 to 6
- point_weight: bfloat16 [256, 256], replicated, may hold values from -0.375 to 0.375
- point_bias: float32 [256], replicated, may hold values from -3 to 3
- spec_real: bfloat16 [128, 256, 256], P('len'), may hold values from -0.25 to 0.25
- spec_imag: bfloat16 [128, 256, 256], P('len'), may hold values from -0.25 to 0.25
- junc_weight: bfloat16 [256, 256], replicated, may hold values from -0.375 to 0.375
- junc_bias: float32 [256], replicated, may hold values from -3 to 3
- inlet_ids: int32 [512], replicated, may hold values from 0 to 511
- outlet_ids: int32 [512], replicated, may hold values from 0 to 511
Outputs:
- outputs: bfloat16 [512, 2048, 256], P(('len', 'pipe'))
- grad_inputs: bfloat16 [512, 2048, 256], P(('len', 'pipe'))
- grad_real: float32 [128, 256, 256], P('len')
- grad_imag: float32 [128, 256, 256], P('len')
All inputs are finite; a program needn't handle non-finite values.
Results may differ from a plain program's by a relative error of at most 0.015.
Values may be sent and summed in bfloat16 or wider, within the bound.
A program may use at most 64 MiB of HBM per device.

v0:
```python
import math

import jax
import jax.numpy as jnp
from jax import lax
from jax.sharding import PartitionSpec as P

COUPLING = 0.125


def tables(cell_count, mode_count):
    position = lax.broadcasted_iota(jnp.int32, (mode_count, cell_count), 1)
    frequency = lax.broadcasted_iota(jnp.int32, (mode_count, cell_count), 0)
    product_index = frequency * position % cell_count
    angles = product_index.astype(jnp.float32) * (2.0 * math.pi / cell_count)
    norm_scale = 1.0 / math.sqrt(cell_count)
    cosine = jnp.cos(angles) * norm_scale
    sine_table = jnp.sin(angles) * norm_scale
    doubled = jnp.where(frequency == 0, 1.0, 2.0)
    forward = (
        jnp.stack([cosine, -sine_table], axis=1)
        .reshape(2 * mode_count, cell_count)
        .astype(jnp.bfloat16)
    )
    inverse = jnp.transpose(
        jnp.stack([doubled * cosine, -doubled * sine_table], axis=1).reshape(
            2 * mode_count, cell_count
        )
    ).astype(jnp.bfloat16)
    return (forward, inverse)


def spectral_blocks(spec_real, spec_imag):
    upper = jnp.concatenate([spec_real, spec_imag], axis=2)
    lower = jnp.concatenate([-spec_imag, spec_real], axis=2)
    return jnp.concatenate([upper, lower], axis=1)


def activate(values):
    return jax.nn.gelu(values, approximate=True)


def silu_slope(values):
    sigmoid_part = jax.nn.sigmoid(values)
    return sigmoid_part * (1.0 + values * (1.0 - sigmoid_part))


def to_modes(field):
    return lax.all_to_all(field, "len", split_axis=1, concat_axis=0, tiled=True)


def from_modes(field):
    return lax.all_to_all(field, "len", split_axis=0, concat_axis=1, tiled=True)


def junction_pass(partial_value, rowwise, carried):
    summed_rows = lax.psum(partial_value, ("len", "pipe"))
    return rowwise(summed_rows, carried)


def body(
    inputs,
    cotangent,
    point_weight,
    point_bias,
    spec_real,
    spec_imag,
    junc_weight,
    junc_bias,
    inlet_ids,
    outlet_ids,
):
    per_dev, cell_count, channels = inputs.shape
    len_count = lax.axis_size("len")
    mode_count = spec_real.shape[0] * len_count
    junc_count = inlet_ids.shape[0]
    forward, inverse = tables(cell_count, mode_count)
    blocks = spectral_blocks(spec_real, spec_imag)
    start = (lax.axis_index("len") * lax.axis_size("pipe") + lax.axis_index("pipe")) * per_dev
    my_inlets = lax.dynamic_slice_in_dim(inlet_ids, start, per_dev)
    my_outlets = lax.dynamic_slice_in_dim(outlet_ids, start, per_dev)
    junction_iota = lax.broadcasted_iota(jnp.int32, (per_dev, junc_count), 1)
    in_hot = (my_inlets[:, None] == junction_iota).astype(jnp.bfloat16)
    out_hot = (my_outlets[:, None] == junction_iota).astype(jnp.bfloat16)
    spectra = jnp.einsum("kl,plc->pkc", forward, inputs, preferred_element_type=jnp.float32).astype(
        jnp.bfloat16
    )
    mode_rows = to_modes(spectra.reshape(per_dev, mode_count, 2, channels))
    mode_rows = mode_rows.reshape(mode_rows.shape[0], -1, 2 * channels)
    mixed = jnp.einsum(
        "pmk,mkn->pmn", mode_rows, blocks, preferred_element_type=jnp.float32
    ).astype(jnp.bfloat16)
    returned_modes = from_modes(mixed.reshape(mixed.shape[0], -1, 2, channels)).reshape(
        per_dev, 2 * mode_count, channels
    )

    def forward_rows(summed_rows, carried):
        junc_act = (
            jnp.dot(
                summed_rows.astype(jnp.bfloat16), junc_weight, preferred_element_type=jnp.float32
            )
            + junc_bias
        )
        return (jax.nn.silu(junc_act).astype(jnp.bfloat16), junc_act)

    def backward_rows(summed_rows, carried):
        act_grad = (summed_rows * silu_slope(carried)).astype(jnp.bfloat16)
        return (
            jnp.dot(act_grad, junc_weight.T, preferred_element_type=jnp.float32).astype(
                jnp.bfloat16
            ),
            carried,
        )

    partial_value = jnp.dot(
        in_hot.T, inputs[:, 0, :], preferred_element_type=jnp.float32
    ) + jnp.dot(out_hot.T, inputs[:, -1, :], preferred_element_type=jnp.float32)
    junc_rows, junc_act = junction_pass(partial_value, forward_rows, None)
    cond = COUPLING * (
        jnp.dot(in_hot, junc_rows, preferred_element_type=jnp.float32)
        + jnp.dot(out_hot, junc_rows, preferred_element_type=jnp.float32)
    )
    spectral = jnp.einsum(
        "lk,pkc->plc", inverse, returned_modes, preferred_element_type=jnp.float32
    )
    pre = (spectral + cond[:, None, :]).astype(jnp.bfloat16)
    pointwise = jnp.dot(
        inputs.reshape(-1, channels), point_weight, preferred_element_type=jnp.float32
    ).reshape(inputs.shape)
    summed = pointwise + point_bias + pre.astype(jnp.float32)
    result, pullback = jax.vjp(activate, summed)
    outputs = result.astype(jnp.bfloat16)
    grad_total = pullback(cotangent.astype(jnp.float32))[0].astype(jnp.bfloat16)
    grad_spec = jnp.einsum(
        "lk,plc->pkc", inverse, grad_total, preferred_element_type=jnp.float32
    ).astype(jnp.bfloat16)
    grad_modes = to_modes(grad_spec.reshape(per_dev, mode_count, 2, channels))
    grad_modes = grad_modes.reshape(grad_modes.shape[0], -1, 2 * channels)
    grad_mixed = jnp.einsum(
        "pmn,mkn->pmk", grad_modes, blocks, preferred_element_type=jnp.float32
    ).astype(jnp.bfloat16)
    weight_terms = jnp.einsum(
        "pmk,pmn->mkn", mode_rows, grad_modes, preferred_element_type=jnp.float32
    )
    real_terms = weight_terms[:, :channels, :channels] + weight_terms[:, channels:, channels:]
    imag_terms = weight_terms[:, :channels, channels:] - weight_terms[:, channels:, :channels]
    grad_real, grad_imag = (
        lax.psum(real_terms.astype(jnp.bfloat16), "pipe").astype(jnp.float32),
        lax.psum(imag_terms.astype(jnp.bfloat16), "pipe").astype(jnp.float32),
    )
    grad_back = from_modes(grad_mixed.reshape(grad_mixed.shape[0], -1, 2, channels)).reshape(
        per_dev, 2 * mode_count, channels
    )
    grad_cells = jnp.einsum("kl,pkc->plc", forward, grad_back, preferred_element_type=jnp.float32)
    grad_cond = jnp.sum(grad_total, axis=1, dtype=jnp.float32)
    in_wide = in_hot.astype(jnp.float32)
    out_wide = out_hot.astype(jnp.float32)
    partial_grad = COUPLING * (
        jnp.dot(in_wide.T, grad_cond, precision=lax.Precision.HIGHEST)
        + jnp.dot(out_wide.T, grad_cond, precision=lax.Precision.HIGHEST)
    )
    sums_grad, unused = junction_pass(partial_grad, backward_rows, junc_act)
    end_first = jnp.dot(in_hot, sums_grad, preferred_element_type=jnp.float32)
    end_last = jnp.dot(out_hot, sums_grad, preferred_element_type=jnp.float32)
    grad_cells = grad_cells.at[:, 0, :].add(end_first).at[:, -1, :].add(end_last)
    spread = grad_cells.astype(jnp.bfloat16)
    grad_local = jnp.dot(
        grad_total.reshape(-1, channels), point_weight.T, preferred_element_type=jnp.float32
    ).reshape(inputs.shape)
    grad_inputs = (grad_local + spread.astype(jnp.float32)).astype(jnp.bfloat16)
    return (outputs, grad_inputs, grad_real, grad_imag)


def solution(mesh):
    placed = (
        P(("len", "pipe"), None, None),
        P(("len", "pipe"), None, None),
        P(),
        P(),
        P("len", None, None),
        P("len", None, None),
        P(),
        P(),
        P(),
        P(),
    )
    return jax.shard_map(
        body,
        mesh=mesh,
        in_specs=placed,
        out_specs=(
            P(("len", "pipe"), None, None),
            P(("len", "pipe"), None, None),
            P("len", None, None),
            P("len", None, None),
        ),
        check_vma=False,
    )
```

profile of v0, /device:TPU:1, one launch (start us, length us, event | category | flops | bytes accessed | tf_op | source)
XLA Modules:
  0.0 740.4 jit_solution(12216176334191740046)
XLA Ops:
  7.2 0.0 copy-start
  7.2 4.3 negate_convert_fusion
  11.5 0.1 pad_maximum_fusion
  11.6 1.1 copy.32
  12.7 0.4 convert_element_type.146
  13.2 0.0 copy-start.14
  13.2 0.4 fusion.18
  13.7 0.7 reshape.383
  14.4 20.6 %all-to-all-start = ((bf16[1,128,2,256]{3,2,0,1:T(2,128)(2,1)}), bf16[1,128,2,256]{3,2,0,1:T(2,128)(2,1)S(1)}, u32[]{:S(2)}, u32[]{:S(2)}) async-start(bf16[1,128,2,256]{3,2,0,1:T(2,128)(2,1)} %bitcast.6), calls=%async_computation | async-start | bytes 262144 | tf_op jit(solution)/shard_map/all_to_all | solution.py:49
  35.0 1.3 dynamic_slice.6
  36.3 0.6 compare_convert_fusion.1
  37.0 1.2 dynamic_slice.7
  38.2 0.6 compare_convert_fusion
  38.8 0.2 multiply_add_fusion
  39.0 108.1 %all-reduce.8 = bf16[512,256]{1,0:T(8,128)(2,1)S(1)} all-reduce(f32[512,256]{1,0:T(8,128)S(1)} %multiply_add_fusion), channel_id=1, replica_groups=mesh['len'=128,'pipe'=4] {'len','pipe'}, use_global_device_ids=true, to_apply=%region_0.1 | all-reduce | flops 131072 | bytes 786432 | tf_op jit(solution)/shard_map/psum | solution.py:57
  147.1 4.4 multiply_convert_fusion.1
  151.5 1.0 multiply_convert_fusion.5
  152.6 0.7 iota_compare_fusion.1
  153.3 0.1 fusion.41
  153.5 0.1 pad_maximum_fusion.1
  153.6 0.3 convolution_convert_fusion.2
  154.0 0.8 copy.34
  154.8 13.4 %all-to-all-start.1 = ((bf16[128,1,2,256]{3,2,1,0:T(2,128)(2,1)}), bf16[128,1,2,256]{3,2,1,0:T(2,128)(2,1)}, u32[]{:S(2)}, u32[]{:S(2)}) async-start(bf16[128,1,2,256]{3,2,1,0:T(2,128)(2,1)} %copy.34), calls=%async_computation.1 | async-start | bytes 262144 | tf_op jit(solution)/shard_map/all_to_all | solution.py:53
  168.1 0.6 iota_compare_fusion
  168.7 1.1 copy.35
  169.8 0.4 convert_element_type.154
  170.3 0.0 copy-start.4
  170.3 0.1 fusion.42
  170.5 14.6 %all-to-all-done.1 = bf16[128,1,2,256]{3,2,1,0:T(2,128)(2,1)} async-done(((bf16[128,1,2,256]{3,2,1,0:T(2,128)(2,1)}), bf16[128,1,2,256]{3,2,1,0:T(2,128)(2,1)}, u32[]{:S(2)}, u32[]{:S(2)}) %all-to-all-start.1) | async-done | bytes 131104 | tf_op jit(solution)/shard_map/all_to_all | solution.py:53
  185.1 1.0 reshape.386
  186.0 0.0 copy-start.11
  186.1 0.6 fusion.7
  186.6 0.6 copy-done.11
  187.3 3.0 convert_reduce_fusion
  190.3 1.0 copy-done.1
  191.2 0.4 fusion.19
  191.7 0.7 reshape.393
  192.4 7.1 all-to-all-start.2
  199.5 0.0 all-reduce.5.cloned.1.call-start
  199.5 1.2 convert_add_fusion
  200.7 1.0 multiply_multiply_fusion.2
  201.7 0.0 all-reduce.5.cloned.1.call-update
  201.7 15.3 %all-to-all-done.2 = bf16[1,128,2,256]{3,2,0,1:T(2,128)(2,1)S(1)} async-done(((bf16[1,128,2,256]{3,2,0,1:T(2,128)(2,1)}), bf16[1,128,2,256]{3,2,0,1:T(2,128)(2,1)S(1)}, u32[]{:S(2)}, u32[]{:S(2)}) %all-to-all-start.2) | async-done | bytes 131104 | tf_op jit(solution)/shard_map/all_to_all | solution.py:49
  217.0 0.3 convolution_convert_fusion.1
  217.4 0.3 convolution_bitcast_fusion.2
  217.7 0.8 copy.38
  218.5 6.9 all-to-all-start.3
  225.4 0.0 all-reduce.7.cloned.1.call-start
  225.4 0.8 fusion.33
  226.2 0.0 all-reduce.7.cloned.1.call-update
  226.2 438.2 %all-reduce.5.cloned.1.call-done = f32[512,256]{1,0:T(8,128)} async-done(((f32[512,256]{1,0:T(8,128)}), f32[512,256]{1,0:T(8,128)}) %all-reduce.5.cloned.1.call-update) | async-done | bytes 524304 | tf_op jit(solution)/shard_map/psum | solution.py:57
  664.4 1.4 convolution_convert_fusion
  665.8 0.1 fusion.44
  666.0 53.9 %all-reduce.7.cloned.1.call-done = (bf16[1,256,256]{2,1,0:T(8,128)(2,1)}, bf16[1,256,256]{2,1,0:T(8,128)(2,1)}) async-done(((bf16[1,256,256]{2,1,0:T(8,128)(2,1)}, bf16[1,256,256]{2,1,0:T(8,128)(2,1)}), (bf16[1,256,256]{2,1,0:T(8,128)(2,1)}, bf16[1,256,256]{2,1,0:T(8,128)(2,1)})) %all-reduce.7.cloned.1.call-update) | async-done | bytes 262160 | tf_op jit(solution)/shard_map/psum | solution.py:148
  719.8 1.6 convert_element_type.176
  721.5 1.6 convert_element_type.178
  723.1 0.7 reshape.396
  723.8 1.4 fusion.43
  725.1 0.1 slice_reduce_fusion
  725.3 1.8 copy.39
  727.1 1.3 scatter-add.6
  728.4 0.8 fusion.20
  729.2 1.3 scatter-add.9
  730.6 3.0 fusion.4
  (44 shorter events, 0.2 us)
Async XLA Ops:
  7.2 179.5 %copy-start = (bf16[256,256]{1,0:T(8,128)(2,1)S(1)}, bf16[256,256]{1,0:T(8,128)(2,1)}, u32[]{:S(2)}) copy-start(bf16[256,256]{1,0:T(8,128)(2,1)} %param.16) | copy-start | bytes 393220
  11.6 1.5 copy-start.3
  13.2 138.3 %copy-start.14 = (bf16[256,256]{1,0:T(8,128)(2,1)S(1)}, bf16[256,256]{1,0:T(8,128)(2,1)}, u32[]{:S(2)}) copy-start(bf16[256,256]{1,0:T(8,128)(2,1)} %param.20) | copy-start | bytes 393220
  13.2 138.3 %copy-start.16 = (f32[256]{0:T(256)S(1)}, f32[256]{0:T(256)}, u32[]{:S(2)}) copy-start(f32[256]{0:T(256)} %param.21) | copy-start | bytes 3076
  14.4 139.2 %all-to-all-start = ((bf16[1,128,2,256]{3,2,0,1:T(2,128)(2,1)}), bf16[1,128,2,256]{3,2,0,1:T(2,128)(2,1)S(1)}, u32[]{:S(2)}, u32[]{:S(2)}) async-start(bf16[1,128,2,256]{3,2,0,1:T(2,128)(2,1)} %bitcast.6), calls=%async_computation | async-start | bytes 262144 | tf_op jit(solution)/shard_map/all_to_all | solution.py:49
  147.1 6.1 copy-start.7
  152.6 1.0 copy-start.12
  153.3 0.7 copy-start.9
  153.6 15.1 %copy-start.5 = (bf16[16,8,2,256]{3,1,2,0:T(8,128)(2,1)}, bf16[16,8,2,256]{3,1,2,0:T(8,128)(2,1)S(1)}, u32[]{:S(2)}) copy-start(bf16[16,8,2,256]{3,1,2,0:T(8,128)(2,1)S(1)} %copy.41) | copy-start | bytes 393220
  154.8 30.3 %all-to-all-start.1 = ((bf16[128,1,2,256]{3,2,1,0:T(2,128)(2,1)}), bf16[128,1,2,256]{3,2,1,0:T(2,128)(2,1)}, u32[]{:S(2)}, u32[]{:S(2)}) async-start(bf16[128,1,2,256]{3,2,1,0:T(2,128)(2,1)} %copy.34), calls=%async_computation.1 | async-start | bytes 262144 | tf_op jit(solution)/shard_map/all_to_all | solution.py:53
  170.3 16.3 %copy-start.4 = (bf16[1,2048,256]{2,1,0:T(8,128)(2,1)S(1)}, bf16[1,2048,256]{2,1,0:T(8,128)(2,1)}, u32[]{:S(2)}) copy-start(bf16[1,2048,256]{2,1,0:T(8,128)(2,1)} %param.14) | copy-start | bytes 3145732
  170.3 16.3 %copy-start.17 = (f32[256]{0:T(256)S(1)}, f32[256]{0:T(256)}, u32[]{:S(2)}) copy-start(f32[256]{0:T(256)} %param.17) | copy-start | bytes 3076
  186.0 1.2 copy-start.11
  190.3 1.0 copy-start.1
  190.3 26.7 %copy-start.8 = (bf16[1,256,256]{2,1,0:T(8,128)(2,1)S(1)}, bf16[1,256,256]{2,1,0:T(8,128)(2,1)}, u32[]{:S(2)}) copy-start(bf16[1,256,256]{2,1,0:T(8,128)(2,1)} %param.19) | copy-start | bytes 393220
  190.3 26.7 %copy-start.10 = (bf16[1,256,256]{2,1,0:T(8,128)(2,1)S(1)}, bf16[1,256,256]{2,1,0:T(8,128)(2,1)}, u32[]{:S(2)}) copy-start(bf16[1,256,256]{2,1,0:T(8,128)(2,1)} %copy-done.9) | copy-start | bytes 393220
  190.3 26.7 %copy-start.13 = (bf16[1,256,256]{2,1,0:T(8,128)(2,1)S(1)}, bf16[1,256,256]{2,1,0:T(8,128)(2,1)}, u32[]{:S(2)}) copy-start(bf16[1,256,256]{2,1,0:T(8,128)(2,1)} %param.18) | copy-start | bytes 393220
  191.7 25.7 %copy-start.6 = (bf16[16,8,2,256]{3,1,2,0:T(8,128)(2,1)S(1)}, bf16[16,8,2,256]{3,1,2,0:T(8,128)(2,1)}, u32[]{:S(2)}) copy-start(bf16[16,8,2,256]{3,1,2,0:T(8,128)(2,1)} %copy-done.5) | copy-start | bytes 393220
  192.4 24.6 %all-to-all-start.2 = ((bf16[1,128,2,256]{3,2,0,1:T(2,128)(2,1)}), bf16[1,128,2,256]{3,2,0,1:T(2,128)(2,1)S(1)}, u32[]{:S(2)}, u32[]{:S(2)}) async-start(bf16[1,128,2,256]{3,2,0,1:T(2,128)(2,1)} %bitcast.24), calls=%async_computation.2 | async-start | bytes 262144 | tf_op jit(solution)/shard_map/all_to_all | solution.py:49
  199.5 465.0 %all-reduce.5.cloned.1.call-start = ((), (), s32[]{:S(2)}) async-start(), calls=%async_computation.4 | async-start | bytes 1048576 | tf_op jit(solution)/shard_map/psum | solution.py:57
  217.3 447.1 %copy-start.15 = (bf16[256,256]{1,0:T(8,128)(2,1)S(1)}, bf16[256,256]{1,0:T(8,128)(2,1)}, u32[]{:S(2)}) copy-start(bf16[256,256]{1,0:T(8,128)(2,1)} %param.20) | copy-start | bytes 393220
  217.4 447.1 %copy-start.18 = (f32[512,256]{1,0:T(8,128)S(1)}, f32[512,256]{1,0:T(8,128)}, u32[]{:S(2)}) copy-start(f32[512,256]{1,0:T(8,128)} %get-tuple-element.38) | copy-start | bytes 1572868
  218.5 504.6 %all-to-all-start.3 = ((bf16[128,1,2,256]{3,2,1,0:T(2,128)(2,1)}), bf16[128,1,2,256]{3,2,1,0:T(2,128)(2,1)S(1)}, u32[]{:S(2)}, u32[]{:S(2)}) async-start(bf16[128,1,2,256]{3,2,1,0:T(2,128)(2,1)} %copy.38), calls=%async_computation.3 | async-start | bytes 262144 | tf_op jit(solution)/shard_map/all_to_all | solution.py:53
  225.4 494.5 %all-reduce.7.cloned.1.call-start = ((), (), s32[]{:S(2)}) async-start(), calls=%async_computation.5 | async-start | bytes 524288 | tf_op jit(solution)/shard_map/psum | solution.py:148
  725.3 5.3 copy-start.2
Sparse Core Ops, SparseCore 0:
  205.7 458.6 all-reduce.4
  667.5 52.2 all-reduce.6
where the time goes:
time: 742 us; the launch traced here: 740 us
  waiting for transfers between devices  522 us (70%)
  blocking collectives  108 us (15%)
  starting transfers between devices  47.9 us (6%)
  other arithmetic  17.7 us (2%)
  local copies, waits for them, and re-layouts  16.5 us (2%)
  between operations  14.6 us (2%)
  matrix products  13.5 us (2%)
    psum x1, waiting for transfers between devices, junction_pass(): summed_rows = lax.psum(partial_value, ('len', 'pipe'))  438 us
    psum x1, blocking collectives, junction_pass(): summed_rows = lax.psum(partial_value, ('len', 'pipe'))  108 us
    psum x1, waiting for transfers between devices, body(): lax.psum(real_terms.astype(jnp.bfloat16), 'pipe').astype(jnp.float32)  53.9 us
    all_to_all x2, starting transfers between devices, to_modes(): return lax.all_to_all(field, 'len', split_axis=1, concat_axis=0, tiled=True)  27.6 us
    all_to_all x2, starting transfers between devices, from_modes(): return lax.all_to_all(field, 'len', split_axis=0, concat_axis=1, tiled=True)  20.2 us
    all_to_all x2, waiting for transfers between devices, to_modes(): return lax.all_to_all(field, 'len', split_axis=1, concat_axis=0, tiled=True)  15.3 us
  transfers between devices with their start and end apart: 6, of which 4 were waited for; matrix products, arithmetic and copies ran while one was open for 3% of the time, Pallas kernels for 0%

commit v1 on v0

--- a/solution.py
+++ b/solution.py
@@ -53,11 +53,6 @@
     return lax.all_to_all(field, "len", split_axis=0, concat_axis=1, tiled=True)
 
 
-def junction_pass(partial_value, rowwise, carried):
-    summed_rows = lax.psum(partial_value, ("len", "pipe"))
-    return rowwise(summed_rows, carried)
-
-
 def body(
     inputs,
     cotangent,
@@ -79,9 +74,12 @@
     start = (lax.axis_index("len") * lax.axis_size("pipe") + lax.axis_index("pipe")) * per_dev
     my_inlets = lax.dynamic_slice_in_dim(inlet_ids, start, per_dev)
     my_outlets = lax.dynamic_slice_in_dim(outlet_ids, start, per_dev)
-    junction_iota = lax.broadcasted_iota(jnp.int32, (per_dev, junc_count), 1)
-    in_hot = (my_inlets[:, None] == junction_iota).astype(jnp.bfloat16)
-    out_hot = (my_outlets[:, None] == junction_iota).astype(jnp.bfloat16)
+    mine = jnp.concatenate([my_inlets, my_outlets])[:, None]
+    in_match = mine == inlet_ids[None, :]
+    out_match = mine == outlet_ids[None, :]
+    end_rows = lax.all_gather(
+        jnp.stack([inputs[:, 0, :], inputs[:, -1, :]]), ("len", "pipe"), axis=1, tiled=True
+    )
     spectra = jnp.einsum("kl,plc->pkc", forward, inputs, preferred_element_type=jnp.float32).astype(
         jnp.bfloat16
     )
@@ -94,32 +92,15 @@
         per_dev, 2 * mode_count, channels
     )
 
-    def forward_rows(summed_rows, carried):
-        junc_act = (
-            jnp.dot(
-                summed_rows.astype(jnp.bfloat16), junc_weight, preferred_element_type=jnp.float32
-            )
-            + junc_bias
-        )
-        return (jax.nn.silu(junc_act).astype(jnp.bfloat16), junc_act)
-
-    def backward_rows(summed_rows, carried):
-        act_grad = (summed_rows * silu_slope(carried)).astype(jnp.bfloat16)
-        return (
-            jnp.dot(act_grad, junc_weight.T, preferred_element_type=jnp.float32).astype(
-                jnp.bfloat16
-            ),
-            carried,
-        )
-
-    partial_value = jnp.dot(
-        in_hot.T, inputs[:, 0, :], preferred_element_type=jnp.float32
-    ) + jnp.dot(out_hot.T, inputs[:, -1, :], preferred_element_type=jnp.float32)
-    junc_rows, junc_act = junction_pass(partial_value, forward_rows, None)
-    cond = COUPLING * (
-        jnp.dot(in_hot, junc_rows, preferred_element_type=jnp.float32)
-        + jnp.dot(out_hot, junc_rows, preferred_element_type=jnp.float32)
+    junc_sums = jnp.dot(
+        in_match.astype(jnp.bfloat16), end_rows[0], preferred_element_type=jnp.float32
+    ) + jnp.dot(out_match.astype(jnp.bfloat16), end_rows[1], preferred_element_type=jnp.float32)
+    junc_act = (
+        jnp.dot(junc_sums.astype(jnp.bfloat16), junc_weight, preferred_element_type=jnp.float32)
+        + junc_bias
     )
+    junc_rows = jax.nn.silu(junc_act).astype(jnp.bfloat16).astype(jnp.float32)
+    cond = COUPLING * (junc_rows[:per_dev] + junc_rows[per_dev:])
     spectral = jnp.einsum(
         "lk,pkc->plc", inverse, returned_modes, preferred_element_type=jnp.float32
     )
@@ -145,23 +126,26 @@
     real_terms = weight_terms[:, :channels, :channels] + weight_terms[:, channels:, channels:]
     imag_terms = weight_terms[:, :channels, channels:] - weight_terms[:, channels:, :channels]
     grad_real, grad_imag = (
-        lax.psum(real_terms.astype(jnp.bfloat16), "pipe").astype(jnp.float32),
-        lax.psum(imag_terms.astype(jnp.bfloat16), "pipe").astype(jnp.float32),
+        jnp.sum(lax.all_gather(real_terms.astype(jnp.bfloat16), "pipe").astype(jnp.float32), axis=0),
+        jnp.sum(lax.all_gather(imag_terms.astype(jnp.bfloat16), "pipe").astype(jnp.float32), axis=0),
     )
     grad_back = from_modes(grad_mixed.reshape(grad_mixed.shape[0], -1, 2, channels)).reshape(
         per_dev, 2 * mode_count, channels
     )
     grad_cells = jnp.einsum("kl,pkc->plc", forward, grad_back, preferred_element_type=jnp.float32)
     grad_cond = jnp.sum(grad_total, axis=1, dtype=jnp.float32)
-    in_wide = in_hot.astype(jnp.float32)
-    out_wide = out_hot.astype(jnp.float32)
-    partial_grad = COUPLING * (
-        jnp.dot(in_wide.T, grad_cond, precision=lax.Precision.HIGHEST)
-        + jnp.dot(out_wide.T, grad_cond, precision=lax.Precision.HIGHEST)
+    all_cond = lax.all_gather(grad_cond, ("len", "pipe"), axis=0, tiled=True)
+    junc_grad = COUPLING * jnp.dot(
+        in_match.astype(jnp.float32) + out_match.astype(jnp.float32),
+        all_cond,
+        precision=lax.Precision.HIGHEST,
     )
-    sums_grad, unused = junction_pass(partial_grad, backward_rows, junc_act)
-    end_first = jnp.dot(in_hot, sums_grad, preferred_element_type=jnp.float32)
-    end_last = jnp.dot(out_hot, sums_grad, preferred_element_type=jnp.float32)
+    act_grad = (junc_grad * silu_slope(junc_act)).astype(jnp.bfloat16)
+    sums_grad = jnp.dot(act_grad, junc_weight.T, preferred_element_type=jnp.float32).astype(
+        jnp.bfloat16
+    )
+    end_first = sums_grad[:per_dev].astype(jnp.float32)
+    end_last = sums_grad[per_dev:].astype(jnp.float32)
     grad_cells = grad_cells.at[:, 0, :].add(end_first).at[:, -1, :].add(end_last)
     spread = grad_cells.astype(jnp.bfloat16)
     grad_local = jnp.dot(

time: 742 us -> 530 us (0.71)
  waiting for transfers between devices: 522 us -> 13.1 us
  blocking collectives: 108 us -> 414 us
  between operations: 14.6 us -> 1.03 us
  starting transfers between devices: 47.9 us -> 55.8 us
    psum x2 -> x0, waiting for transfers between devices: 492 us -> none  [the longest x1 438 us: junction_pass(): summed_rows = lax.psum(partial_value, ('len', 'pipe'))]
    all_gather x0 -> x4, blocking collectives: none -> 414 us  [the longest x1 197 us: body(): lax.all_gather(jnp.stack([inputs[:, 0, :], inputs[:, -1, :]]), ('len', 'p...]
    psum x1 -> x0, blocking collectives: 108 us -> none  [junction_pass(): summed_rows = lax.psum(partial_value, ('len', 'pipe'))]
    all_to_all x2, waiting for transfers between devices: 15.3 us -> 0.01 us  [to_modes(): return lax.all_to_all(field, 'len', split_axis=1, concat_axis=0, tiled=True)]
    all_to_all x2, starting transfers between devices: 20.2 us -> 28.3 us  [from_modes(): return lax.all_to_all(field, 'len', split_axis=0, concat_axis=1, tiled=True)]
  transfers between devices with their start and end apart: 6 -> 4, of which waited for: 4 -> 1; matrix products, arithmetic and copies ran while one was open for 3% -> 3% of each run, Pallas kernels for 0% -> 0%
where the time goes in v1:
time: 530 us; the launch traced here: 525 us
  blocking collectives  414 us (78%)
  starting transfers between devices  55.8 us (11%)
  local copies, waits for them, and re-layouts  16.1 us (3%)
  waiting for transfers between devices  13.1 us (2%)
  other arithmetic  12.6 us (2%)
  matrix products  12.3 us (2%)
    all_gather x1, blocking collectives, body(): lax.all_gather(jnp.stack([inputs[:, 0, :], inputs[:, -1, :]]), ('len', 'p...  197 us
    all_gather x1, blocking collectives, body(): all_cond = lax.all_gather(grad_cond, ('len', 'pipe'), axis=0, tiled=True)  196 us
    all_to_all x2, starting transfers between devices, from_modes(): return lax.all_to_all(field, 'len', split_axis=0, concat_axis=1, tiled=True)  28.3 us
    all_to_all x2, starting transfers between devices, to_modes(): return lax.all_to_all(field, 'len', split_axis=1, concat_axis=0, tiled=True)  27.5 us
    all_to_all x2, waiting for transfers between devices, from_modes(): return lax.all_to_all(field, 'len', split_axis=0, concat_axis=1, tiled=True)  13.1 us
    all_gather x1, blocking collectives, body(): lax.all_gather(real_terms.astype(jnp.bfloat16), 'pipe').astype(jnp.float32)  10.8 us
  transfers between devices with their start and end apart: 4, of which 1 were waited for; matrix products, arithmetic and copies ran while one was open for 3% of the time, Pallas kernels for 0%

profile of v1, /device:TPU:1, one launch (start us, length us, event | category | flops | bytes accessed | tf_op | source)
XLA Modules:
  0.0 525.2 jit_solution(12464476966603268177)
XLA Ops:
  0.6 0.0 copy-start
  0.6 4.3 negate_convert_fusion
  5.0 0.1 pad_maximum_fusion
  5.1 0.0 copy-start.3
  5.1 1.1 copy.48
  6.2 0.0 copy-start.10
  6.2 0.0 copy-start.11
  6.2 0.4 convert_element_type.155
  6.7 0.0 copy-start.6
  6.7 0.4 fusion.18
  7.1 0.7 reshape.318
  7.8 20.6 %all-to-all-start = ((bf16[1,128,2,256]{3,2,0,1:T(2,128)(2,1)}), bf16[1,128,2,256]{3,2,0,1:T(2,128)(2,1)S(1)}, u32[]{:S(2)}, u32[]{:S(2)}) async-start(bf16[1,128,2,256]{3,2,0,1:T(2,128)(2,1)} %bitcast.6), calls=%async_computation | async-start | bytes 262144 | tf_op jit(solution)/shard_map/all_to_all | solution.py:49
  28.5 0.6 dynamic_slice.6
  29.1 0.6 dynamic_slice.7
  29.7 0.0 copy-start.8
  29.7 1.4 pad_add_fusion
  31.1 4.4 multiply_convert_fusion.1
  35.5 0.0 copy-start.15
  35.5 0.1 pad_maximum_fusion.1
  35.6 197.2 %all_gather.18 = bf16[2,512,256]{2,0,1:T(2,128)(2,1)S(1)} all-gather(bf16[2,1,256]{2,0,1:T(2,128)(2,1)S(1)} %pad_maximum_fusion.2), channel_id=1, replica_groups=mesh['len'=128,'pipe'=4] {'len','pipe'}, dimensions={1}, use_global_device_ids=true | all-gather | bytes 525312 | tf_op jit(solution)/shard_map/all_gather | solution.py:80
  232.8 1.5 fusion.64
  234.3 0.0 all-to-all-done
  234.4 0.3 convolution_convert_fusion.1
  234.7 0.8 copy.50
  235.5 14.4 %all-to-all-start.1 = ((bf16[128,1,2,256]{3,2,1,0:T(2,128)(2,1)}), bf16[128,1,2,256]{3,2,1,0:T(2,128)(2,1)}, u32[]{:S(2)}, u32[]{:S(2)}) async-start(bf16[128,1,2,256]{3,2,1,0:T(2,128)(2,1)} %copy.50), calls=%async_computation.1 | async-start | bytes 262144 | tf_op jit(solution)/shard_map/all_to_all | solution.py:53
  249.9 0.8 fusion.39
  250.7 1.1 copy.51
  251.8 0.4 convert_element_type.163
  252.2 0.0 copy-start.4
  252.2 1.5 fusion.54
  253.8 13.1 %all-to-all-done.1 = bf16[128,1,2,256]{3,2,1,0:T(2,128)(2,1)} async-done(((bf16[128,1,2,256]{3,2,1,0:T(2,128)(2,1)}), bf16[128,1,2,256]{3,2,1,0:T(2,128)(2,1)}, u32[]{:S(2)}, u32[]{:S(2)}) %all-to-all-start.1) | async-done | bytes 131104 | tf_op jit(solution)/shard_map/all_to_all | solution.py:53
  266.8 1.0 reshape.321
  267.8 0.0 copy-start.14
  267.8 0.6 fusion.7
  268.4 0.6 copy-done.14
  269.0 3.7 convert_reduce_fusion
  272.7 1.0 copy-done.1
  273.7 0.4 fusion.19
  274.1 0.7 reshape.324
  274.8 6.9 %all-to-all-start.2 = ((bf16[1,128,2,256]{3,2,0,1:T(2,128)(2,1)}), bf16[1,128,2,256]{3,2,0,1:T(2,128)(2,1)S(1)}, u32[]{:S(2)}, u32[]{:S(2)}) async-start(bf16[1,128,2,256]{3,2,0,1:T(2,128)(2,1)} %bitcast.19), calls=%async_computation.2 | async-start | bytes 262144 | tf_op jit(solution)/shard_map/all_to_all | solution.py:49
  281.8 196.1 %all-gather.3 = f32[512,1,256]{2,1,0:T(1,128)S(1)} all-gather(f32[1,1,256]{2,1,0:T(1,128)S(1)} %bitcast.136), channel_id=2, replica_groups=mesh['len'=128,'pipe'=4] {'len','pipe'}, dimensions={0}, use_global_device_ids=true | all-gather | bytes 525312 | tf_op jit(solution)/shard_map/all_gather | solution.py:137
  477.8 0.3 fusion.22
  478.2 0.0 copy-done.5
  478.2 0.1 convolution_convert_fusion.4
  478.4 0.0 all-to-all-done.2
  478.5 0.3 convolution_convert_fusion
  478.8 0.3 convolution_bitcast_fusion.2
  479.1 0.8 copy.58
  479.9 13.9 %all-to-all-start.3 = ((bf16[128,1,2,256]{3,2,1,0:T(2,128)(2,1)}), bf16[128,1,2,256]{3,2,1,0:T(2,128)(2,1)S(1)}, u32[]{:S(2)}, u32[]{:S(2)}) async-start(bf16[128,1,2,256]{3,2,1,0:T(2,128)(2,1)} %copy.58), calls=%async_computation.3 | async-start | bytes 262144 | tf_op jit(solution)/shard_map/all_to_all | solution.py:53
  493.8 0.1 fusion.37
  493.8 10.8 %all-gather.1 = bf16[4,256,256]{2,1,0:T(8,128)(2,1)S(1)} all-gather(bf16[1,256,256]{2,1,0:T(8,128)(2,1)S(1)} %get-tuple-element.32), channel_id=3, replica_groups=mesh['len'=128,'pipe'=4] {'pipe'}, dimensions={0}, use_global_device_ids=true | all-gather | bytes 655360 | tf_op jit(solution)/shard_map/all_gather | solution.py:129
  504.6 0.8 convert_reduce_fusion.2
  505.4 10.3 %all-gather.2 = bf16[4,256,256]{2,1,0:T(8,128)(2,1)S(1)} all-gather(bf16[1,256,256]{2,1,0:T(8,128)(2,1)S(1)} %get-tuple-element.31), channel_id=4, replica_groups=mesh['len'=128,'pipe'=4] {'pipe'}, dimensions={0}, use_global_device_ids=true | all-gather | bytes 655360 | tf_op jit(solution)/shard_map/all_gather | solution.py:130
  515.6 0.8 convert_reduce_fusion.1
  516.4 0.0 all-to-all-done.3
  516.4 0.1 reshape.327
  516.5 0.5 fusion.67
  516.9 0.1 slice_reduce_fusion
  517.0 0.0 copy-start.2
  517.1 1.8 copy.59
  518.9 1.3 scatter-add.6
  520.2 0.7 fusion.56
  520.9 1.3 scatter-add.9
  522.2 3.0 fusion.4
  (30 shorter events, 0.2 us)
Async XLA Ops:
  0.6 267.8 %copy-start = (bf16[256,256]{1,0:T(8,128)(2,1)S(1)}, bf16[256,256]{1,0:T(8,128)(2,1)}, u32[]{:S(2)}) copy-start(bf16[256,256]{1,0:T(8,128)(2,1)} %param.16) | copy-start | bytes 393220
  5.1 1.6 copy-start.3
  6.2 22.3 %copy-start.10 = (s32[512]{0:T(512)S(1)}, s32[512]{0:T(512)}, u32[]{:S(2)}) copy-start(s32[512]{0:T(512)} %param.22) | copy-start | bytes 6148
  6.2 22.9 %copy-start.11 = (s32[512]{0:T(512)S(1)}, s32[512]{0:T(512)}, u32[]{:S(2)}) copy-start(s32[512]{0:T(512)} %param.23) | copy-start | bytes 6148
  6.7 23.0 %copy-start.6 = (bf16[1,256,256]{2,1,0:T(8,128)(2,1)S(1)}, bf16[1,256,256]{2,1,0:T(8,128)(2,1)}, u32[]{:S(2)}) copy-start(bf16[1,256,256]{2,1,0:T(8,128)(2,1)} %param.19) | copy-start | bytes 393220
  7.8 226.5 %all-to-all-start = ((bf16[1,128,2,256]{3,2,0,1:T(2,128)(2,1)}), bf16[1,128,2,256]{3,2,0,1:T(2,128)(2,1)S(1)}, u32[]{:S(2)}, u32[]{:S(2)}) async-start(bf16[1,128,2,256]{3,2,0,1:T(2,128)(2,1)} %bitcast.6), calls=%async_computation | async-start | bytes 262144 | tf_op jit(solution)/shard_map/all_to_all | solution.py:49
  29.7 204.7 %copy-start.8 = (bf16[1,256,256]{2,1,0:T(8,128)(2,1)}, bf16[1,256,256]{2,1,0:T(8,128)(2,1)S(1)}, u32[]{:S(2)}) copy-start(bf16[1,256,256]{2,1,0:T(8,128)(2,1)S(1)} %neg.22) | copy-start | bytes 393220
  31.1 221.1 %copy-start.12 = (s32[2]{0:T(128)}, s32[2]{0:T(128)S(1)}, u32[]{:S(2)}) copy-start(s32[2]{0:T(128)S(1)} %pad_add_fusion) | copy-start | bytes 28
  35.5 198.9 %copy-start.15 = (bf16[1,256,256]{2,1,0:T(8,128)(2,1)S(1)}, bf16[1,256,256]{2,1,0:T(8,128)(2,1)}, u32[]{:S(2)}) copy-start(bf16[1,256,256]{2,1,0:T(8,128)(2,1)} %param.18) | copy-start | bytes 393220
  235.5 31.3 %all-to-all-start.1 = ((bf16[128,1,2,256]{3,2,1,0:T(2,128)(2,1)}), bf16[128,1,2,256]{3,2,1,0:T(2,128)(2,1)}, u32[]{:S(2)}, u32[]{:S(2)}) async-start(bf16[128,1,2,256]{3,2,1,0:T(2,128)(2,1)} %copy.50), calls=%async_computation.1 | async-start | bytes 262144 | tf_op jit(solution)/shard_map/all_to_all | solution.py:53
  252.2 16.2 %copy-start.4 = (bf16[1,2048,256]{2,1,0:T(8,128)(2,1)S(1)}, bf16[1,2048,256]{2,1,0:T(8,128)(2,1)}, u32[]{:S(2)}) copy-start(bf16[1,2048,256]{2,1,0:T(8,128)(2,1)} %param.14) | copy-start | bytes 3145732
  267.8 1.2 copy-start.14
  272.7 1.0 copy-start.1
  272.7 205.1 %copy-start.13 = (s32[2]{0:T(128)S(1)}, s32[2]{0:T(128)}, u32[]{:S(2)}) copy-start(s32[2]{0:T(128)} %copy-done.12) | copy-start | bytes 28
  272.7 205.5 %copy-start.5 = (bf16[256,256]{1,0:T(8,128)(2,1)S(1)}, bf16[256,256]{1,0:T(8,128)(2,1)}, u32[]{:S(2)}) copy-start(bf16[256,256]{1,0:T(8,128)(2,1)} %param.20) | copy-start | bytes 393220
  273.7 204.8 %copy-start.7 = (bf16[1,256,256]{2,1,0:T(8,128)(2,1)S(1)}, bf16[1,256,256]{2,1,0:T(8,128)(2,1)}, u32[]{:S(2)}) copy-start(bf16[1,256,256]{2,1,0:T(8,128)(2,1)} %param.19) | copy-start | bytes 393220
  273.7 204.8 %copy-start.9 = (bf16[1,256,256]{2,1,0:T(8,128)(2,1)S(1)}, bf16[1,256,256]{2,1,0:T(8,128)(2,1)}, u32[]{:S(2)}) copy-start(bf16[1,256,256]{2,1,0:T(8,128)(2,1)} %copy-done.8) | copy-start | bytes 393220
  273.7 204.8 %copy-start.16 = (bf16[1,256,256]{2,1,0:T(8,128)(2,1)S(1)}, bf16[1,256,256]{2,1,0:T(8,128)(2,1)}, u32[]{:S(2)}) copy-start(bf16[1,256,256]{2,1,0:T(8,128)(2,1)} %param.18) | copy-start | bytes 393220
  274.8 203.5 %all-to-all-start.2 = ((bf16[1,128,2,256]{3,2,0,1:T(2,128)(2,1)}), bf16[1,128,2,256]{3,2,0,1:T(2,128)(2,1)S(1)}, u32[]{:S(2)}, u32[]{:S(2)}) async-start(bf16[1,128,2,256]{3,2,0,1:T(2,128)(2,1)} %bitcast.19), calls=%async_computation.2 | async-start | bytes 262144 | tf_op jit(solution)/shard_map/all_to_all | solution.py:49
  479.9 36.6 %all-to-all-start.3 = ((bf16[128,1,2,256]{3,2,1,0:T(2,128)(2,1)}), bf16[128,1,2,256]{3,2,1,0:T(2,128)(2,1)S(1)}, u32[]{:S(2)}, u32[]{:S(2)}) async-start(bf16[128,1,2,256]{3,2,1,0:T(2,128)(2,1)} %copy.58), calls=%async_computation.3 | async-start | bytes 262144 | tf_op jit(solution)/shard_map/all_to_all | solution.py:53
  517.0 5.2 copy-start.2

commit v2 on v1

v2 whole, which is shorter than its diff:
```python
import functools
import math

import jax
import jax.numpy as jnp
from jax import lax
from jax.experimental import pallas as pl
from jax.experimental.pallas import tpu as pltpu
from jax.sharding import PartitionSpec as P

COUPLING = 0.125
LINE = 16
CORES = 2
TILE = 256
MESH = pl.DeviceIdType.MESH
BF = jnp.bfloat16
F32 = jnp.float32
GELU_A = math.sqrt(2.0 / math.pi)
GELU_B = GELU_A * 0.044715


def far_first(count):
    return sorted(range(1, count), key=lambda k: (-min(k, count - k), k))


def dot(left, right):
    return jnp.dot(left, right, preferred_element_type=F32)


def dot_nt(left, right):
    return lax.dot_general(left, right, (((1,), (1,)), ((), ())), preferred_element_type=F32)


def dot_tn(left, right):
    return lax.dot_general(left, right, (((0,), (0,)), ((), ())), preferred_element_type=F32)


def turn_cos(index, cell_count):
    half, quarter = cell_count // 2, cell_count // 4
    away = jnp.abs(index - half)
    folded = jnp.minimum(away, half - away)
    x = folded.astype(F32) * (2.0 * math.pi / cell_count)
    y = x * x
    value = jnp.full_like(y, 1.0 / math.factorial(12))
    for power in (10, 8, 6, 4, 2, 0):
        sign = 1.0 if power % 4 == 0 else -1.0
        value = value * y + sign / math.factorial(power)
    return jnp.where(away > quarter, value, -value)


def mode_of(row, line):
    group = row // (2 * line)
    spot = (row // 2) % line
    return ((group // CORES) * line + spot) * CORES + group % CORES


def base_tables(row, col, cell_count, line):
    mode = mode_of(row, line)
    index = mode * col + (cell_count // 4) * (row % 2)
    scale = 1.0 / math.sqrt(cell_count)
    cosine = turn_cos(index % cell_count, cell_count) * scale
    sine = turn_cos((index + 3 * (cell_count // 4)) % cell_count, cell_count) * scale
    return cosine, sine


def shift_factors(row, step, steps, line):
    index = (mode_of(row, line) * step) % steps
    return turn_cos(index, steps), turn_cos((index + 3 * (steps // 4)) % steps, steps)


def kernel_body(
    dims,
    x_hbm, cot_hbm, pw_ref, pb_ref, sr_ref, si_ref, jw_ref, jb_ref, in_ref, out_ref,
    y_hbm, gi_hbm, gr_hbm, gm_hbm,
    xv, cotv, ftab, ttab, pointv, gtv, localv, yv, giv, acc,
    send_g, recv_g, send_z, recv_z,
    own_z, ag_z, own_g, ag_g, ag_x,
    wfull, wsend, wrecv, wtot, grout,
    perm_p, perm_q, sel_f, sel_b, condv, jactv, rowv,
    load_sem, out_sem, ssem, rsem,
):
    line, groups, width, pipes = dims["line"], dims["groups"], dims["width"], dims["pipes"]
    cells, chans, rows = dims["cells"], dims["chans"], dims["rows"]
    chunks = cells // TILE
    len_me, x_me = lax.axis_index("len"), lax.axis_index("pipe")
    c_me = len_me % CORES
    z_me = (len_me // CORES) % line
    y_me = len_me // (CORES * line)
    g_me = y_me * CORES + c_me

    def len_of(group, spot):
        return ((group // CORES) * line + spot) * CORES + group % CORES

    def at_g(k):
        group = (g_me + k) % groups
        return group, {"len": len_of(group, z_me), "pipe": x_me}

    def at_z(k):
        spot = (z_me + k) % line
        return spot, {"len": len_of(g_me, spot), "pipe": x_me}

    def at_x(k):
        column = (x_me + k) % width
        return column, {"len": len_me, "pipe": column}

    peers = {"g": (at_g, groups), "z": (at_z, line), "x": (at_x, width)}

    def send(axis, phase, source, target):
        at, count = peers[axis]
        for k in far_first(count):
            spot, device = at(k)
            pltpu.make_async_remote_copy(
                src_ref=source(spot),
                dst_ref=target,
                send_sem=ssem.at[phase],
                recv_sem=rsem.at[phase],
                device_id=device,
                device_id_type=MESH,
            ).start()

    def drain(sem, phase, blocks, count):
        part = blocks.at[pl.ds(0, count - 1)]
        pltpu.make_async_copy(part, part, sem.at[phase]).wait()

    load_x = pltpu.make_async_copy(x_hbm, xv, load_sem.at[0])
    load_cot = pltpu.make_async_copy(cot_hbm, cotv, load_sem.at[1])
    load_x.start()
    load_cot.start()

    barrier = pltpu.get_barrier_semaphore()
    for at, count in peers.values():
        for k in range(1, count):
            pl.semaphore_signal(barrier, inc=1, device_id=at(k)[1], device_id_type=MESH)

    row_id = lax.broadcasted_iota(jnp.int32, (rows, TILE), 0)
    col_id = lax.broadcasted_iota(jnp.int32, (rows, TILE), 1)
    base_cos, base_sin = base_tables(row_id, col_id, cells, line)
    localv[0:rows, :] = base_cos
    localv[rows : 2 * rows, :] = base_sin
    row_one = lax.broadcasted_iota(jnp.int32, (rows, 1), 0)
    acc[...] = jnp.zeros_like(acc)
    load_x.wait()

    def spectra_step(k, carry):
        turn_c, turn_s = shift_factors(row_one, k, chunks, line)
        table = (localv[0:rows, :] * turn_c - localv[rows : 2 * rows, :] * turn_s).astype(BF)
        ftab[k] = table
        acc[...] += dot(table, xv[pl.ds(k * TILE, TILE), :])
        return carry

    lax.fori_loop(0, chunks, spectra_step, 0)
    send_g[0] = acc[...].astype(BF).reshape(groups, 2 * line, chans)
    pl.semaphore_wait(barrier, (groups - 1) + (line - 1) + (width - 1))

    def hop_g(phase, slot):
        recv_g[slot, g_me] = send_g[slot, g_me]
        send("g", phase, lambda spot: send_g.at[slot, spot], recv_g.at[slot, g_me])

    def hop_z(phase, slot):
        recv_z[slot, z_me] = send_z[slot, z_me]
        send("z", phase, lambda spot: send_z.at[slot, spot], recv_z.at[slot, z_me])

    def to_line(slot):
        block = dot(perm_p[...], recv_g[slot].reshape(rows, chans)).astype(BF)
        send_z[slot] = block.reshape(line, 2 * groups, chans)

    def to_group(slot):
        block = dot_tn(perm_p[...], recv_z[slot].reshape(rows, chans)).astype(BF)
        send_g[slot] = block.reshape(groups, 2 * line, chans)

    hop_g(0, 0)

    def gather_z(phase, slot, first, second):
        part = lax.broadcasted_iota(jnp.int32, (2, chans), 0)
        own_z[slot] = jnp.where(part == 0, first, second).astype(BF)
        ag_z[slot, z_me] = own_z[slot]
        send("z", phase, lambda spot: own_z.at[slot], ag_z.at[slot, z_me])

    def gather_g(phase, slot):
        for spot in range(line):
            rowv[2 * spot : 2 * spot + 2, :] = ag_z[slot, spot].astype(F32)
        own_g[slot] = rowv[...].astype(BF)
        ag_g[slot, g_me] = own_g[slot]
        send("g", phase, lambda spot: own_g.at[slot], ag_g.at[slot, g_me])

    def gather_x(phase, slot):
        ag_x[slot, x_me] = ag_g[slot]
        send("x", phase, lambda spot: ag_g.at[slot], ag_x.at[slot, x_me])

    first_row = xv[0:16, :].astype(F32)[0:1, :]
    last_row = xv[cells - 16 : cells, :].astype(F32)[15:16, :]
    gather_z(1, 0, first_row, last_row)

    to_row = lax.broadcasted_iota(jnp.int32, (rows, rows), 0)
    from_row = lax.broadcasted_iota(jnp.int32, (rows, rows), 1)
    spot_of, group_of = to_row // (2 * groups), (to_row // 2) % groups
    wanted = group_of * (2 * line) + spot_of * 2 + to_row % 2
    perm_p[...] = (from_row == wanted).astype(F32).astype(BF)
    swapped = jnp.where(to_row % 2 == 0, to_row + 1, to_row - 1)
    sign = jnp.where(to_row % 2 == 0, -1.0, 1.0)
    perm_q[...] = jnp.where(from_row == swapped, sign, 0.0).astype(BF)

    drain(rsem, 0, recv_g.at[0], groups)
    to_line(0)
    hop_z(2, 0)

    ids_in, ids_out = in_ref[...].astype(F32), out_ref[...].astype(F32)
    place = lax.broadcasted_iota(jnp.int32, (1, pipes), 1)
    here = place == len_me * width + x_me
    mine_in = jnp.sum(jnp.where(here, ids_in, 0.0), axis=1, keepdims=True)
    mine_out = jnp.sum(jnp.where(here, ids_out, 0.0), axis=1, keepdims=True)
    which = lax.broadcasted_iota(jnp.int32, (8, pipes), 0)

    def matches(ids):
        pair = jnp.where(which == 0, (ids == mine_in).astype(F32), (ids == mine_out).astype(F32))
        return jnp.where(which < 2, pair, 0.0).astype(BF)

    pipe_row = lax.broadcasted_iota(jnp.int32, (pipes, 2 * pipes), 0)
    entry = lax.broadcasted_iota(jnp.int32, (1, 2 * pipes), 1)
    part = entry % 2
    spot_e = (entry // 2) % line
    group_e = (entry // (2 * line)) % groups
    column_e = entry // (2 * line * groups)
    pipe_e = len_of(group_e, spot_e) * width + column_e
    hot_first = jnp.where(pipe_row == jnp.where(part == 0, pipe_e, -1), 1.0, 0.0).astype(BF)
    hot_last = jnp.where(pipe_row == jnp.where(part == 1, pipe_e, -1), 1.0, 0.0).astype(BF)
    match_in, match_out = matches(ids_in), matches(ids_out)
    sel_f[...] = (dot(match_in, hot_first) + dot(match_out, hot_last)).astype(BF)
    both = (match_in.astype(F32) + match_out.astype(F32)).astype(BF)
    sel_b[...] = (dot(both, hot_first) + dot(both, hot_last)).astype(BF)

    drain(rsem, 1, ag_z.at[0], line)
    gather_g(3, 0)

    def point_step(k, carry):
        part_rows = pl.ds(k * TILE, TILE)
        pointv[part_rows, :] = dot(xv[part_rows, :], pw_ref[...]) + pb_ref[...]
        return carry

    lax.fori_loop(0, chunks, point_step, 0)

    drain(rsem, 3, ag_g.at[0], groups)
    gather_x(4, 0)

    drain(rsem, 2, recv_z.at[0], line)
    data = recv_z[0].reshape(rows, chans)
    turned = dot(perm_q[...], data).astype(BF)
    mixed = dot(data, sr_ref[...]) + dot(turned, si_ref[...])
    send_z[1] = mixed.astype(BF).reshape(line, 2 * groups, chans)
    hop_z(5, 1)

    cell_id = lax.broadcasted_iota(jnp.int32, (TILE, rows), 0)
    mode_id = lax.broadcasted_iota(jnp.int32, (TILE, rows), 1)
    side_cos, side_sin = base_tables(mode_id, cell_id, cells, line)
    localv[0:TILE, :] = side_cos
    localv[TILE : 2 * TILE, :] = side_sin
    col_one = lax.broadcasted_iota(jnp.int32, (1, rows), 1)

    def side_step(k, carry):
        turn_c, turn_s = shift_factors(col_one, k, chunks, line)
        ttab[k] = (localv[0:TILE, :] * turn_c - localv[TILE : 2 * TILE, :] * turn_s).astype(BF)
        return carry

    lax.fori_loop(0, chunks, side_step, 0)

    drain(rsem, 4, ag_x.at[0], width)
    sums = dot(sel_f[...], ag_x[0].reshape(2 * pipes, chans))
    junc_act = dot(sums.astype(BF), jw_ref[...]) + jb_ref[...]
    jactv[...] = junc_act
    junc_rows = (junc_act * jax.nn.sigmoid(junc_act)).astype(BF).astype(F32)
    condv[...] = COUPLING * (junc_rows[0:1, :] + junc_rows[1:2, :])

    drain(rsem, 5, recv_z.at[1], line)
    to_group(1)
    hop_g(6, 1)
    weight_row = lax.broadcasted_iota(jnp.int32, (rows, 1), 0)
    doubled = jnp.where(mode_of(weight_row, line) == 0, 1.0, 2.0)
    load_cot.wait()
    drain(rsem, 6, recv_g.at[1], groups)
    scaled = (recv_g[1].reshape(rows, chans).astype(F32) * doubled).astype(BF)
    send_g[2] = scaled.reshape(groups, 2 * line, chans)

    acc[...] = jnp.zeros_like(acc)

    def gelu_step(k, total):
        part_rows = pl.ds(k * TILE, TILE)
        spectral = dot(ttab[k], send_g[2].reshape(rows, chans))
        pre = (spectral + condv[...]).astype(BF).astype(F32)
        s = pointv[part_rows, :] + pre
        square = s * s
        bent = jnp.tanh(s * (GELU_A + GELU_B * square))
        half = 0.5 + 0.5 * bent
        yv[part_rows, :] = (s * half).astype(BF)
        slope = half + (0.5 * s) * (1.0 - bent * bent) * (GELU_A + (3.0 * GELU_B) * square)
        grad = (cotv[part_rows, :].astype(F32) * slope).astype(BF)
        gtv[part_rows, :] = grad
        acc[...] += dot(ftab[k], grad)
        pltpu.make_async_copy(yv.at[part_rows], y_hbm.at[part_rows], out_sem.at[0]).start()
        return total + jnp.sum(grad.astype(F32), axis=0, keepdims=True)

    grad_cond = lax.fori_loop(0, chunks, gelu_step, jnp.zeros((1, chans), F32))
    send_g[3] = (acc[...] * doubled).astype(BF).reshape(groups, 2 * line, chans)
    hop_g(7, 3)
    high = grad_cond.astype(BF).astype(F32)
    gather_z(8, 1, high, grad_cond - high)

    drain(rsem, 7, recv_g.at[3], groups)
    to_line(3)
    hop_z(9, 3)

    drain(rsem, 8, ag_z.at[1], line)
    gather_g(10, 1)

    def local_step(k, carry):
        part_rows = pl.ds(k * TILE, TILE)
        localv[part_rows, :] = dot_nt(gtv[part_rows, :], pw_ref[...])
        return carry

    lax.fori_loop(0, chunks, local_step, 0)
    drain(rsem, 10, ag_g.at[1], groups)
    gather_x(11, 1)

    drain(rsem, 9, recv_z.at[3], line)
    grads = recv_z[3].reshape(rows, chans)
    flipped = dot_tn(perm_q[...], grads).astype(BF)
    back = dot_nt(grads, sr_ref[...]) + dot_nt(flipped, si_ref[...])
    send_z[2] = back.astype(BF).reshape(line, 2 * groups, chans)
    hop_z(12, 2)

    data = recv_z[0].reshape(rows, chans)
    real = dot_tn(data, grads)
    imag = dot_tn(data, flipped)
    share = chans // width
    for column in range(width):
        cut = slice(column * share, (column + 1) * share)
        wfull[column, 0] = real[cut, :]
        wfull[column, 1] = imag[cut, :]
    wsend[...] = wfull[...].astype(BF)
    send("x", 13, lambda spot: wsend.at[spot], wrecv.at[x_me])

    drain(rsem, 11, ag_x.at[1], width)
    junc_grad = COUPLING * dot(sel_b[...], ag_x[1].reshape(2 * pipes, chans))
    junc_act = jactv[...]
    gate = jax.nn.sigmoid(junc_act)
    act_grad = (junc_grad * (gate * (1.0 + junc_act * (1.0 - gate)))).astype(BF)
    jactv[...] = dot_nt(act_grad, jw_ref[...]).astype(BF).astype(F32)

    drain(rsem, 13, wrecv, width)
    wrecv[x_me] = jnp.zeros(wrecv.shape[1:], BF)
    total = wfull[x_me]
    for column in range(width):
        total = total + wrecv[column].astype(F32)
    wtot[x_me] = total.astype(BF)
    send("x", 14, lambda spot: wtot.at[x_me], wtot.at[x_me])

    drain(rsem, 12, recv_z.at[2], line)
    to_group(2)
    hop_g(15, 2)

    drain(rsem, 14, wtot, width)
    for column in range(width):
        cut = slice(column * share, (column + 1) * share)
        grout[0, cut, :] = wtot[column, 0].astype(F32)
        grout[1, cut, :] = wtot[column, 1].astype(F32)
    put_real = pltpu.make_async_copy(grout.at[0], gr_hbm, out_sem.at[1])
    put_imag = pltpu.make_async_copy(grout.at[1], gm_hbm, out_sem.at[2])
    put_real.start()
    put_imag.start()

    drain(rsem, 15, recv_g.at[2], groups)

    def final_step(k, ends):
        part_rows = pl.ds(k * TILE, TILE)
        spread = dot(ttab[k], recv_g[2].reshape(rows, chans))
        if ends is not None:
            spread = spread + ends
        giv[part_rows, :] = (localv[part_rows, :] + spread.astype(BF).astype(F32)).astype(BF)
        pltpu.make_async_copy(giv.at[part_rows], gi_hbm.at[part_rows], out_sem.at[3]).start()

    tile_row = lax.broadcasted_iota(jnp.int32, (TILE, chans), 0)
    final_step(0, jnp.where(tile_row == 0, jactv[0:1, :], 0.0))

    def final_loop(k, carry):
        final_step(k, None)
        return carry

    lax.fori_loop(1, chunks - 1, final_loop, 0)
    final_step(chunks - 1, jnp.where(tile_row == TILE - 1, jactv[1:2, :], 0.0))

    for phase, blocks, count in (
        (0, recv_g.at[0], groups), (1, ag_z.at[0], line), (2, recv_z.at[0], line),
        (3, ag_g.at[0], groups), (4, ag_x.at[0], width), (5, recv_z.at[1], line),
        (6, recv_g.at[1], groups), (7, recv_g.at[3], groups), (8, ag_z.at[1], line),
        (9, recv_z.at[3], line), (10, ag_g.at[1], groups), (11, ag_x.at[1], width),
        (12, recv_z.at[2], line), (13, wrecv, width), (14, wtot, width),
        (15, recv_g.at[2], groups),
    ):
        drain(ssem, phase, blocks, count)
    pltpu.make_async_copy(yv, y_hbm, out_sem.at[0]).wait()
    put_real.wait()
    put_imag.wait()
    pltpu.make_async_copy(giv, gi_hbm, out_sem.at[3]).wait()


def body(
    inputs, cotangent, point_weight, point_bias, spec_real, spec_imag,
    junc_weight, junc_bias, inlet_ids, outlet_ids,
):
    per_dev, cells, chans = inputs.shape
    len_count, width = lax.axis_size("len"), lax.axis_size("pipe")
    line, groups = LINE, len_count // LINE
    rows, pipes = 2 * len_count, inlet_ids.shape[0]
    dims = dict(
        line=line, groups=groups, width=width, pipes=pipes, cells=cells, chans=chans, rows=rows
    )
    share = chans // width
    vm = pltpu.VMEM
    anywhere = pl.BlockSpec(memory_space=pl.ANY)
    inside = pl.BlockSpec(memory_space=pltpu.VMEM)
    y, gi, gr, gm = pl.pallas_call(
        functools.partial(kernel_body, dims),
        out_shape=(
            jax.ShapeDtypeStruct((cells, chans), BF),
            jax.ShapeDtypeStruct((cells, chans), BF),
            jax.ShapeDtypeStruct((chans, chans), F32),
            jax.ShapeDtypeStruct((chans, chans), F32),
        ),
        in_specs=[anywhere] * 2 + [inside] * 8,
        out_specs=(anywhere,) * 4,
        scratch_shapes=[
            vm((cells, chans), BF), vm((cells, chans), BF),
            vm((cells // TILE, rows, TILE), BF), vm((cells // TILE, TILE, rows), BF),
            vm((cells, chans), F32), vm((cells, chans), BF), vm((cells, chans), F32),
            vm((cells, chans), BF), vm((cells, chans), BF), vm((rows, chans), F32),
            vm((4, groups, 2 * line, chans), BF), vm((4, groups, 2 * line, chans), BF),
            vm((4, line, 2 * groups, chans), BF), vm((4, line, 2 * groups, chans), BF),
            vm((2, 2, chans), BF), vm((2, line, 2, chans), BF),
            vm((2, 2 * line, chans), BF), vm((2, groups, 2 * line, chans), BF),
            vm((2, width, groups, 2 * line, chans), BF),
            vm((width, 2, share, chans), F32), vm((width, 2, share, chans), BF),
            vm((width, 2, share, chans), BF), vm((width, 2, share, chans), BF),
            vm((2, chans, chans), F32),
            vm((rows, rows), BF), vm((rows, rows), BF),
            vm((8, 2 * pipes), BF), vm((8, 2 * pipes), BF),
            vm((1, chans), F32), vm((8, chans), F32), vm((2 * line, chans), F32),
            pltpu.SemaphoreType.DMA((2,)), pltpu.SemaphoreType.DMA((4,)),
            pltpu.SemaphoreType.DMA((16,)), pltpu.SemaphoreType.DMA((16,)),
        ],
        compiler_params=pltpu.CompilerParams(
            collective_id=0, has_side_effects=True, vmem_limit_bytes=48 << 20
        ),
        name="operator_step",
    )(
        inputs[0], cotangent[0], point_weight, point_bias[None, :], spec_real[0], spec_imag[0],
        junc_weight, junc_bias[None, :], inlet_ids[None, :], outlet_ids[None, :],
    )
    return y[None], gi[None], gr[None], gm[None]


def solution(mesh):
    split = P(("len", "pipe"), None, None)
    modes = P("len", None, None)
    return jax.shard_map(
        body,
        mesh=mesh,
        in_specs=(split, split, P(), P(), modes, modes, P(), P(), P(), P()),
        out_specs=(split, split, modes, modes),
        check_vma=False,
    )
```

time: 530 us -> 90.2 us (0.17)
  blocking collectives: 414 us -> 0 us
  Pallas kernels: 0 us -> 79.1 us
  starting transfers between devices: 55.8 us -> 0 us
  waiting for transfers between devices: 13.1 us -> 0 us
  other arithmetic: 12.6 us -> 0 us
  matrix products: 12.3 us -> 0 us
  local copies, waits for them, and re-layouts: 16.1 us -> 10.1 us
    all_gather x4 -> x0, blocking collectives: 414 us -> none  [the longest x1 197 us: body(): lax.all_gather(jnp.stack([inputs[:, 0, :], inputs[:, -1, :]]), ('len', 'p...]
    pallas_call x0 -> x1, Pallas kernels: none -> 79.1 us  [body(): pl.pallas_call(functools.partial(kernel_body, dims), out_shape=(jax.Shape...]
    all_to_all x4 -> x0, starting transfers between devices: 55.8 us -> none  [the longest x2 28.3 us: from_modes(): return lax.all_to_all(field, 'len', split_axis=0, concat_axis=1, tiled=True)]
    all_to_all x4 -> x0, waiting for transfers between devices: 13.1 us -> none  [the longest x2 13.1 us: from_modes(): return lax.all_to_all(field, 'len', split_axis=0, concat_axis=1, tiled=True)]
    dot_general x13 -> x0, matrix products: 12.3 us -> none  [the longest x1 3.67 us: body(): jnp.dot(inputs.reshape(-1, channels), point_weight, preferred_element_typ...]
    another operation x5 -> x0, other arithmetic: 8.9 us -> none
    unnamed x37 -> x24, local copies, waits for them, and re-layouts: 1.79 us -> 10.1 us
  transfers between devices with their start and end apart: 4 -> 0, of which waited for: 1 -> 0; matrix products, arithmetic and copies ran while one was open for 3% -> 0% of each run, Pallas kernels for 0% -> 0%
where the time goes in v2:
time: 90.2 us; the launch traced here: 89.9 us
  Pallas kernels  79.1 us (88%)
  local copies, waits for them, and re-layouts  10.1 us (11%)
    pallas_call x1, Pallas kernels, body(): pl.pallas_call(functools.partial(kernel_body, dims), out_shape=(jax.Shape...  79.1 us
    unnamed x24, local copies, waits for them, and re-layouts  10.1 us

profile of v2, /device:TPU:1, one launch (start us, length us, event | category | flops | bytes accessed | tf_op | source)
XLA Modules:
  0.0 89.9 jit_solution(5054282616364986697)
XLA Ops:
  0.6 0.0 copy-start.9
  0.6 0.0 copy-start.7
  0.7 0.0 copy-start.6
  0.7 0.0 copy-start.8
  0.7 0.6 copy-done.9
  1.3 0.0 copy-done.7
  1.3 0.0 copy-done.6
  1.3 0.0 copy-done.8
  1.4 0.0 copy-start
  1.4 1.2 %copy-done = bf16[1,2048,256]{2,1,0:T(8,128)(2,1)S(1)} copy-done((bf16[1,2048,256]{2,1,0:T(8,128)(2,1)S(1)}, bf16[1,2048,256]{2,1,0:T(8,128)(2,1)}, u32[]{:S(2)}) %copy-start) | copy-done | bytes 1048600
  2.6 0.0 copy-start.1
  2.6 1.2 %copy-done.1 = bf16[1,2048,256]{2,1,0:T(8,128)(2,1)S(1)} copy-done((bf16[1,2048,256]{2,1,0:T(8,128)(2,1)S(1)}, bf16[1,2048,256]{2,1,0:T(8,128)(2,1)}, u32[]{:S(2)}) %copy-start.1) | copy-done | bytes 1048600
  3.8 0.0 copy-start.2
  3.8 0.9 %copy-done.2 = bf16[256,256]{1,0:T(8,128)(2,1)S(1)} copy-done((bf16[256,256]{1,0:T(8,128)(2,1)S(1)}, bf16[256,256]{1,0:T(8,128)(2,1)}, u32[]{:S(2)}) %copy-start.2) | copy-done | bytes 131096
  4.7 0.0 copy-start.3
  4.7 0.9 %copy-done.3 = bf16[1,256,256]{2,1,0:T(8,128)(2,1)S(1)} copy-done((bf16[1,256,256]{2,1,0:T(8,128)(2,1)S(1)}, bf16[1,256,256]{2,1,0:T(8,128)(2,1)}, u32[]{:S(2)}) %copy-start.3) | copy-done | bytes 131096
  5.6 0.0 copy-start.4
  5.6 0.9 %copy-done.4 = bf16[1,256,256]{2,1,0:T(8,128)(2,1)S(1)} copy-done((bf16[1,256,256]{2,1,0:T(8,128)(2,1)S(1)}, bf16[1,256,256]{2,1,0:T(8,128)(2,1)}, u32[]{:S(2)}) %copy-start.4) | copy-done | bytes 131096
  6.5 0.0 copy-start.5
  6.5 0.9 %copy-done.5 = bf16[256,256]{1,0:T(8,128)(2,1)S(1)} copy-done((bf16[256,256]{1,0:T(8,128)(2,1)S(1)}, bf16[256,256]{1,0:T(8,128)(2,1)}, u32[]{:S(2)}) %copy-start.5) | copy-done | bytes 131096
  7.4 79.1 %operator_step.1 = (bf16[2048,256]{1,0:T(8,128)(2,1)S(1)}, bf16[2048,256]{1,0:T(8,128)(2,1)S(1)}, f32[256,256]{1,0:T(8,128)S(1)}, f32[256,256]{1,0:T(8,128)S(1)}) custom-call(bf16[2048,256]{1,0:T(8,128)(2,1)S(1)} %bitcast.12, bf16[2048,256]{1,0:T(8,128)(2,1)S(1)} %bitcast.13, bf16[256,256]{1,0:T(8,128)(2,1)S(1)} %copy-done.2, f32[1,256]{1,0:T(1,128)S(1)} %bitcast.22, ...), custom_call_target="tpu_custom_call" | custom-call | tf_op jit(solution)/shard_map/operator_step/pallas_call | solution.py:420
  86.5 1.0 %copy.18 = bf16[1,2048,256]{2,1,0:T(8,128)(2,1)} copy(bf16[1,2048,256]{2,1,0:T(8,128)(2,1)S(1)} %bitcast.15) | data formatting | bytes 2097152
  87.5 1.0 %copy.19 = bf16[1,2048,256]{2,1,0:T(8,128)(2,1)} copy(bf16[1,2048,256]{2,1,0:T(8,128)(2,1)S(1)} %bitcast.14) | data formatting | bytes 2097152
  88.5 0.7 copy.20
  89.2 0.7 copy.21
Async XLA Ops:
  0.6 0.7 copy-start.9
  0.6 0.7 copy-start.7
  0.7 0.7 copy-start.6
  0.7 0.7 copy-start.8
  1.4 1.2 %copy-start = (bf16[1,2048,256]{2,1,0:T(8,128)(2,1)S(1)}, bf16[1,2048,256]{2,1,0:T(8,128)(2,1)}, u32[]{:S(2)}) copy-start(bf16[1,2048,256]{2,1,0:T(8,128)(2,1)} %param.10) | copy-start | bytes 3145732
  2.6 1.2 %copy-start.1 = (bf16[1,2048,256]{2,1,0:T(8,128)(2,1)S(1)}, bf16[1,2048,256]{2,1,0:T(8,128)(2,1)}, u32[]{:S(2)}) copy-start(bf16[1,2048,256]{2,1,0:T(8,128)(2,1)} %param.11) | copy-start | bytes 3145732
  3.8 0.9 %copy-start.2 = (bf16[256,256]{1,0:T(8,128)(2,1)S(1)}, bf16[256,256]{1,0:T(8,128)(2,1)}, u32[]{:S(2)}) copy-start(bf16[256,256]{1,0:T(8,128)(2,1)} %pw_ref.1) | copy-start | bytes 393220
  4.7 0.9 %copy-start.3 = (bf16[1,256,256]{2,1,0:T(8,128)(2,1)S(1)}, bf16[1,256,256]{2,1,0:T(8,128)(2,1)}, u32[]{:S(2)}) copy-start(bf16[1,256,256]{2,1,0:T(8,128)(2,1)} %param.14) | copy-start | bytes 393220
  5.6 0.9 %copy-start.4 = (bf16[1,256,256]{2,1,0:T(8,128)(2,1)S(1)}, bf16[1,256,256]{2,1,0:T(8,128)(2,1)}, u32[]{:S(2)}) copy-start(bf16[1,256,256]{2,1,0:T(8,128)(2,1)} %param.15) | copy-start | bytes 393220
  6.5 0.9 %copy-start.5 = (bf16[256,256]{1,0:T(8,128)(2,1)S(1)}, bf16[256,256]{1,0:T(8,128)(2,1)}, u32[]{:S(2)}) copy-start(bf16[256,256]{1,0:T(8,128)(2,1)} %jw_ref.1) | copy-start | bytes 393220

commit v3 on v2

v3 whole, which is shorter than its diff:
```python
import functools
import math

import jax
import jax.numpy as jnp
from jax import lax
from jax.experimental import pallas as pl
from jax.experimental.pallas import tpu as pltpu
from jax.sharding import PartitionSpec as P

COUPLING = 0.125
LINE = 16
CORES = 2
TILE = 256
MESH = pl.DeviceIdType.MESH
BF = jnp.bfloat16
F32 = jnp.float32
GELU_A = math.sqrt(2.0 / math.pi)
GELU_B = GELU_A * 0.044715


def dot(left, right):
    return jnp.dot(left, right, preferred_element_type=F32)


def dot_nt(left, right):
    return lax.dot_general(left, right, (((1,), (1,)), ((), ())), preferred_element_type=F32)


def dot_tn(left, right):
    return lax.dot_general(left, right, (((0,), (0,)), ((), ())), preferred_element_type=F32)


def turn_cos(index, cell_count):
    half, quarter = cell_count // 2, cell_count // 4
    away = jnp.abs(index - half)
    folded = jnp.minimum(away, half - away)
    x = folded.astype(F32) * (2.0 * math.pi / cell_count)
    y = x * x
    value = jnp.full_like(y, 1.0 / math.factorial(12))
    for power in (10, 8, 6, 4, 2, 0):
        sign = 1.0 if power % 4 == 0 else -1.0
        value = value * y + sign / math.factorial(power)
    return jnp.where(away > quarter, value, -value)


def mode_of(row, chips):
    return (row // 2) % chips * CORES + row // (2 * chips)


def base_tables(row, col, cell_count, chips):
    mode = mode_of(row, chips)
    index = mode * col + (cell_count // 4) * (row % 2)
    scale = 1.0 / math.sqrt(cell_count)
    cosine = turn_cos(index % cell_count, cell_count) * scale
    sine = turn_cos((index + 3 * (cell_count // 4)) % cell_count, cell_count) * scale
    return cosine, sine


def shift_factors(row, step, steps, chips):
    index = (mode_of(row, chips) * step) % steps
    return turn_cos(index, steps), turn_cos((index + 3 * (steps // 4)) % steps, steps)


def kernel_body(
    dims,
    x_hbm, cot_hbm, pw_hbm, pb_hbm, sr_hbm, si_hbm, jw_hbm, jb_hbm, in_hbm, out_hbm,
    y_out, gi_out, gr_out, gm_out,
    xv, cotv, pw_ref, pb_ref, sr_ref, si_ref, jw_ref, jb_ref, in_ref, out_ref,
    ftab, ttab, pointv, gtv, localv, yv, giv, acc,
    stage, duo, data, mixd, back, fin,
    own_z, ag_z, fwd_y, fwd_x, fwd_c, bwd_y, bwd_x, bwd_c,
    wfull, wsend, wrecv, wtot, grout,
    perm_q, sel_f, sel_b, scaledv, condv, jactv, rowv,
    load_sem, out_sem, ssem, rsem,
):
    line, ys, width, pipes = dims["line"], dims["ys"], dims["width"], dims["pipes"]
    cells, chans, rows = dims["cells"], dims["chans"], dims["rows"]
    chips = line * ys
    chunks = cells // TILE
    len_me, x_me = lax.axis_index("len"), lax.axis_index("pipe")
    c_me = len_me % CORES
    chip_me = len_me // CORES
    z_me = chip_me % line
    y_me = chip_me // line
    c_other = 1 - c_me

    def chip_at(dy, dz):
        return (y_me + dy) % ys * line + (z_me + dz) % line

    def on_chip(chip):
        return {"len": chip * CORES + c_me, "pipe": x_me}

    def on_column(k):
        return {"len": len_me, "pipe": (x_me + k) % width}

    sibling = {"len": chip_me * CORES + c_other, "pipe": x_me}
    y_order = sorted(range(ys), key=lambda k: -min(k, ys - k))

    def z_step(j):
        return line // 2 + ((j + 1) // 2) * (1 - 2 * (j % 2))

    def put(phase, source, target, device):
        pltpu.make_async_remote_copy(
            src_ref=source, dst_ref=target, send_sem=ssem.at[phase], recv_sem=rsem.at[phase],
            device_id=device, device_id_type=MESH,
        ).start()

    def drain(sem, phase, part):
        pltpu.make_async_copy(part, part, sem.at[phase]).wait()

    def each_chip(action, low, high):
        def step(j, carry):
            for dy in y_order:
                action(chip_at(dy, z_step(j)))
            return carry

        lax.fori_loop(low, min(high, line - 1), step, 0)
        if high == line:
            for dy in y_order[:-1]:
                action(chip_at(dy, 0))

    loads = [
        pltpu.make_async_copy(source, target, load_sem.at[i])
        for i, (source, target) in enumerate((
            (x_hbm, xv), (sr_hbm, sr_ref), (si_hbm, si_ref), (in_hbm, in_ref), (out_hbm, out_ref),
            (pw_hbm, pw_ref), (pb_hbm, pb_ref), (jw_hbm, jw_ref), (jb_hbm, jb_ref), (cot_hbm, cotv),
        ))
    ]
    for load in loads:
        load.start()

    barrier = pltpu.get_barrier_semaphore()

    def greet(device):
        pl.semaphore_signal(barrier, inc=1, device_id=device, device_id_type=MESH)

    each_chip(lambda chip: greet(on_chip(chip)), 0, line)
    for k in range(1, width):
        greet(on_column(k))
    greet(sibling)

    row_id = lax.broadcasted_iota(jnp.int32, (rows, TILE), 0)
    col_id = lax.broadcasted_iota(jnp.int32, (rows, TILE), 1)
    base_cos, base_sin = base_tables(row_id, col_id, cells, chips)
    localv[0:rows, :] = base_cos
    localv[rows : 2 * rows, :] = base_sin
    row_one = lax.broadcasted_iota(jnp.int32, (rows, 1), 0)
    doubled = jnp.where(mode_of(row_one, chips) == 0, 1.0, 2.0)
    acc[...] = jnp.zeros_like(acc)
    loads[0].wait()

    def spectra_step(k, carry):
        turn_c, turn_s = shift_factors(row_one, k, chunks, chips)
        table = (localv[0:rows, :] * turn_c - localv[rows : 2 * rows, :] * turn_s).astype(BF)
        ftab[k] = table
        acc[...] += dot(table, xv[pl.ds(k * TILE, TILE), :])
        return carry

    lax.fori_loop(0, chunks, spectra_step, 0)
    stage[0] = acc[...].astype(BF).reshape(CORES, chips, 2, chans)
    pl.semaphore_wait(barrier, chips - 1 + width - 1 + 1)

    def swap_out(slot, phase):
        put(phase, stage.at[slot, c_other], duo.at[slot, :, c_me], sibling)
        duo[slot, :, c_me] = stage[slot, c_me]

    def chips_out(slot, phase, low, high):
        if low == 0:
            data[slot, chip_me] = duo[slot, chip_me]
        each_chip(
            lambda chip: put(phase, duo.at[slot, chip], data.at[slot, chip_me], on_chip(chip)),
            low, high,
        )

    def chips_back(slot, phase, low, high):
        if low == 0:
            back[slot, chip_me] = mixd[slot, chip_me]
        each_chip(
            lambda chip: put(phase, mixd.at[slot, chip], back.at[slot, chip_me], on_chip(chip)),
            low, high,
        )

    def swap_back(slot, phase):
        put(phase, back.at[slot, :, c_other], fin.at[slot, c_me], sibling)
        fin[slot, c_me] = back[slot, :, c_me]

    others = pl.ds(0, chips - 1)

    def gather_z(slot, phase, first, second):
        part = lax.broadcasted_iota(jnp.int32, (2, chans), 0)
        own_z[slot] = jnp.where(part == 0, first, second).astype(BF)
        ag_z[slot, z_me] = own_z[slot]

        def step(j, carry):
            put(phase, own_z.at[slot], ag_z.at[slot, z_me], on_chip(chip_at(0, z_step(j))))
            return carry

        lax.fori_loop(0, line - 1, step, 0)

    def gather_y(ref, phase, block):
        ref[y_me] = block
        for dy in y_order[:-1]:
            put(phase, ref.at[y_me], ref.at[y_me], on_chip(chip_at(dy, 0)))

    def gather_x(source, ref, phase):
        ref[x_me] = source[...]
        for k in (2, 1, 3):
            put(phase, source, ref.at[x_me], on_column(k))

    swap_out(0, 0)
    first_row = xv[0:16, :].astype(F32)[0:1, :]
    last_row = xv[cells - 16 : cells, :].astype(F32)[15:16, :]
    gather_z(0, 8, first_row, last_row)
    drain(rsem, 0, stage.at[0, 0])
    chips_out(0, 1, 0, line)

    cell_id = lax.broadcasted_iota(jnp.int32, (TILE, rows), 0)
    mode_id = lax.broadcasted_iota(jnp.int32, (TILE, rows), 1)
    side_cos, side_sin = base_tables(mode_id, cell_id, cells, chips)
    localv[0:TILE, :] = side_cos
    localv[TILE : 2 * TILE, :] = side_sin
    col_one = lax.broadcasted_iota(jnp.int32, (1, rows), 1)

    def side_step(k, carry):
        turn_c, turn_s = shift_factors(col_one, k, chunks, chips)
        ttab[k] = (localv[0:TILE, :] * turn_c - localv[TILE : 2 * TILE, :] * turn_s).astype(BF)
        return carry

    lax.fori_loop(0, chunks, side_step, 0)

    to_row = lax.broadcasted_iota(jnp.int32, (rows, rows), 0)
    from_row = lax.broadcasted_iota(jnp.int32, (rows, rows), 1)
    swapped = jnp.where(to_row % 2 == 0, to_row + 1, to_row - 1)
    sign = jnp.where(to_row % 2 == 0, -1.0, 1.0)
    perm_q[...] = jnp.where(from_row == swapped, sign, 0.0).astype(BF)
    for load in loads[1:9]:
        load.wait()

    drain(rsem, 8, ag_z.at[0, pl.ds(0, line - 1)])
    for spot in range(line):
        rowv[2 * spot : 2 * spot + 2, :] = ag_z[0, spot].astype(F32)
    gather_y(fwd_y, 9, rowv[...].astype(BF))

    drain(rsem, 1, data.at[0, others])
    seen = data[0].reshape(rows, chans)
    turned = dot(perm_q[...], seen).astype(BF)
    mixed = dot(seen, sr_ref[...]) + dot(turned, si_ref[...])
    mixd[0] = mixed.astype(BF).reshape(chips, CORES, 2, chans)
    chips_back(0, 2, 0, line)

    drain(rsem, 9, fwd_y.at[pl.ds(0, ys - 1)])
    gather_x(fwd_y, fwd_x, 10)

    ids_in, ids_out = in_ref[...].astype(F32), out_ref[...].astype(F32)
    place = lax.broadcasted_iota(jnp.int32, (1, pipes), 1)
    here = place == len_me * width + x_me
    mine_in = jnp.sum(jnp.where(here, ids_in, 0.0), axis=1, keepdims=True)
    mine_out = jnp.sum(jnp.where(here, ids_out, 0.0), axis=1, keepdims=True)
    which = lax.broadcasted_iota(jnp.int32, (8, pipes), 0)

    def matches(ids):
        pair = jnp.where(which == 0, (ids == mine_in).astype(F32), (ids == mine_out).astype(F32))
        return jnp.where(which < 2, pair, 0.0).astype(BF)

    def pipe_of(index):
        chip = index % chips
        column = (index // chips) % width
        core = jnp.where(index // (chips * width) == 0, c_me, c_other)
        return (chip * CORES + core) * width + column

    match_in, match_out = matches(ids_in), matches(ids_out)
    entry = lax.broadcasted_iota(jnp.int32, (1, 2 * pipes), 1)
    pipe_e = pipe_of(entry // 2)
    pipe_row = lax.broadcasted_iota(jnp.int32, (pipes, 2 * pipes), 0)
    hot_first = jnp.where(pipe_row == jnp.where(entry % 2 == 0, pipe_e, -1), 1.0, 0.0).astype(BF)
    hot_last = jnp.where(pipe_row == jnp.where(entry % 2 == 1, pipe_e, -1), 1.0, 0.0).astype(BF)
    sel_f[...] = (dot(match_in, hot_first) + dot(match_out, hot_last)).astype(BF)
    entry = lax.broadcasted_iota(jnp.int32, (1, pipes), 1)
    pipe_row = lax.broadcasted_iota(jnp.int32, (pipes, pipes), 0)
    hot = jnp.where(pipe_row == pipe_of(entry), 1.0, 0.0).astype(BF)
    sel_b[...] = (dot(match_in, hot) + dot(match_out, hot)).astype(BF)

    def point_step(k, carry):
        part_rows = pl.ds(k * TILE, TILE)
        pointv[part_rows, :] = dot(xv[part_rows, :], pw_ref[...]) + pb_ref[...]
        return carry

    lax.fori_loop(0, chunks, point_step, 0)

    drain(rsem, 10, fwd_x.at[pl.ds(0, width - 1)])
    put(11, fwd_x, fwd_c, sibling)
    drain(rsem, 2, back.at[0, others])
    swap_back(0, 3)

    drain(rsem, 11, fwd_c)
    sums = dot(sel_f[:, 0:pipes], fwd_x[...].reshape(pipes, chans)) + dot(
        sel_f[:, pipes : 2 * pipes], fwd_c[...].reshape(pipes, chans)
    )
    junc_act = dot(sums.astype(BF), jw_ref[...]) + jb_ref[...]
    jactv[...] = junc_act
    junc_rows = (junc_act * jax.nn.sigmoid(junc_act)).astype(BF).astype(F32)
    condv[...] = COUPLING * (junc_rows[0:1, :] + junc_rows[1:2, :])
    loads[9].wait()

    drain(rsem, 3, fin.at[0, 0])
    scaledv[...] = (fin[0].reshape(rows, chans).astype(F32) * doubled).astype(BF)

    acc[...] = jnp.zeros_like(acc)

    def gelu_step(k, total):
        part_rows = pl.ds(k * TILE, TILE)
        spectral = dot(ttab[k], scaledv[...])
        pre = (spectral + condv[...]).astype(BF).astype(F32)
        s = pointv[part_rows, :] + pre
        square = s * s
        half = 0.5 + 0.5 * jnp.tanh(s * (GELU_A + GELU_B * square))
        value = s * half
        yv[part_rows, :] = value.astype(BF)
        slope = half + (value - value * half) * (2.0 * GELU_A + (6.0 * GELU_B) * square)
        grad = (cotv[part_rows, :].astype(F32) * slope).astype(BF)
        gtv[part_rows, :] = grad
        acc[...] += dot(ftab[k], grad)
        return total + jnp.sum(grad.astype(F32), axis=0, keepdims=True)

    grad_cond = lax.fori_loop(0, chunks, gelu_step, jnp.zeros((1, chans), F32))
    stage[1] = (acc[...] * doubled).astype(BF).reshape(CORES, chips, 2, chans)
    swap_out(1, 4)
    high = grad_cond.astype(BF).astype(F32)
    gather_z(1, 12, high, grad_cond - high)
    drain(rsem, 4, stage.at[0, 0])
    chips_out(1, 5, 0, line)
    put_y = pltpu.make_async_copy(yv, y_out, out_sem.at[0])
    put_y.start()

    def local_step(k, carry):
        part_rows = pl.ds(k * TILE, TILE)
        localv[part_rows, :] = dot_nt(gtv[part_rows, :], pw_ref[...])
        return carry

    lax.fori_loop(0, chunks, local_step, 0)

    drain(rsem, 12, ag_z.at[1, pl.ds(0, line - 1)])
    for spot in range(line):
        rowv[spot : spot + 1, :] = jnp.sum(ag_z[1, spot].astype(F32), axis=0, keepdims=True)
    gather_y(bwd_y, 13, rowv[0:line, :].astype(BF))

    drain(rsem, 5, data.at[1, others])
    grads = data[1].reshape(rows, chans)
    flipped = dot_tn(perm_q[...], grads).astype(BF)
    returned = dot_nt(grads, sr_ref[...]) + dot_nt(flipped, si_ref[...])
    mixd[1] = returned.astype(BF).reshape(chips, CORES, 2, chans)
    seen = data[0].reshape(rows, chans)
    real = dot_tn(seen, grads)
    imag = dot_tn(seen, flipped)
    share = chans // width
    for column in range(width):
        cut = slice(column * share, (column + 1) * share)
        wfull[column, 0] = real[cut, :]
        wfull[column, 1] = imag[cut, :]
    wsend[...] = wfull[...].astype(BF)
    for k in (2, 1, 3):
        put(16, wsend.at[(x_me + k) % width], wrecv.at[x_me], on_column(k))
    chips_back(1, 6, 0, line // 2)
    drain(rsem, 13, bwd_y.at[pl.ds(0, ys - 1)])
    gather_x(bwd_y, bwd_x, 14)
    chips_back(1, 6, line // 2, line)

    drain(rsem, 16, wrecv.at[pl.ds(0, width - 1)])
    wrecv[x_me] = jnp.zeros(wrecv.shape[1:], BF)
    total = wfull[x_me]
    for column in range(width):
        total = total + wrecv[column].astype(F32)
    wtot[x_me] = total.astype(BF)
    for k in (2, 1, 3):
        put(17, wtot.at[x_me], wtot.at[x_me], on_column(k))

    drain(rsem, 14, bwd_x.at[pl.ds(0, width - 1)])
    put(15, bwd_x, bwd_c, sibling)
    drain(rsem, 15, bwd_c)
    half_pipes = pipes // 2
    junc_grad = COUPLING * (
        dot(sel_b[:, 0:half_pipes], bwd_x[...].reshape(half_pipes, chans))
        + dot(sel_b[:, half_pipes:pipes], bwd_c[...].reshape(half_pipes, chans))
    )
    junc_act = jactv[...]
    gate = jax.nn.sigmoid(junc_act)
    act_grad = (junc_grad * (gate * (1.0 + junc_act * (1.0 - gate)))).astype(BF)
    jactv[...] = dot_nt(act_grad, jw_ref[...]).astype(BF).astype(F32)

    drain(rsem, 6, back.at[1, others])
    swap_back(1, 7)
    drain(rsem, 7, fin.at[1, 0])

    def final_step(k, ends):
        part_rows = pl.ds(k * TILE, TILE)
        spread = dot(ttab[k], fin[1].reshape(rows, chans))
        if ends is not None:
            spread = spread + ends
        giv[part_rows, :] = (localv[part_rows, :] + spread.astype(BF).astype(F32)).astype(BF)
        pltpu.make_async_copy(giv.at[part_rows], gi_out.at[part_rows], out_sem.at[3]).start()

    tile_row = lax.broadcasted_iota(jnp.int32, (TILE, chans), 0)
    final_step(0, jnp.where(tile_row == 0, jactv[0:1, :], 0.0))

    def final_loop(k, carry):
        final_step(k, None)
        return carry

    lax.fori_loop(1, chunks - 1, final_loop, 0)
    final_step(chunks - 1, jnp.where(tile_row == TILE - 1, jactv[1:2, :], 0.0))

    drain(rsem, 17, wtot.at[pl.ds(0, width - 1)])
    for column in range(width):
        cut = slice(column * share, (column + 1) * share)
        grout[0, cut, :] = wtot[column, 0].astype(F32)
        grout[1, cut, :] = wtot[column, 1].astype(F32)
    put_real = pltpu.make_async_copy(grout.at[0], gr_out, out_sem.at[1])
    put_imag = pltpu.make_async_copy(grout.at[1], gm_out, out_sem.at[2])
    put_real.start()
    put_imag.start()

    for phase, part in (
        (0, stage.at[0, 0]), (1, data.at[0, others]), (2, back.at[0, others]), (3, fin.at[0, 0]),
        (4, stage.at[0, 0]), (5, data.at[1, others]), (6, back.at[1, others]), (7, fin.at[1, 0]),
        (8, ag_z.at[0, pl.ds(0, line - 1)]), (9, fwd_y.at[pl.ds(0, ys - 1)]),
        (10, fwd_x.at[pl.ds(0, width - 1)]), (11, fwd_c),
        (12, ag_z.at[1, pl.ds(0, line - 1)]), (13, bwd_y.at[pl.ds(0, ys - 1)]),
        (14, bwd_x.at[pl.ds(0, width - 1)]), (15, bwd_c),
        (16, wrecv.at[pl.ds(0, width - 1)]), (17, wtot.at[pl.ds(0, width - 1)]),
    ):
        drain(ssem, phase, part)
    put_y.wait()
    put_real.wait()
    put_imag.wait()
    pltpu.make_async_copy(giv, gi_out, out_sem.at[3]).wait()


def deliver(*refs):
    count = (len(refs) - 1) // 2
    copies = [
        pltpu.make_async_copy(refs[i], refs[count + i], refs[-1].at[i]) for i in range(count)
    ]
    for copy in copies:
        copy.start()
    for copy in copies:
        copy.wait()


def body(
    inputs, cotangent, point_weight, point_bias, spec_real, spec_imag,
    junc_weight, junc_bias, inlet_ids, outlet_ids,
):
    per_dev, cells, chans = inputs.shape
    len_count, width = lax.axis_size("len"), lax.axis_size("pipe")
    line, chips = LINE, len_count // CORES
    ys = chips // line
    rows, pipes = 2 * len_count, inlet_ids.shape[0]
    dims = dict(
        line=line, ys=ys, width=width, pipes=pipes, cells=cells, chans=chans, rows=rows
    )
    share = chans // width
    vm = pltpu.VMEM
    far = pl.BlockSpec(memory_space=pltpu.HBM)
    anywhere = pl.BlockSpec(memory_space=pl.ANY)
    results = (
        jax.ShapeDtypeStruct((cells, chans), BF),
        jax.ShapeDtypeStruct((cells, chans), BF),
        jax.ShapeDtypeStruct((chans, chans), F32),
        jax.ShapeDtypeStruct((chans, chans), F32),
    )
    made = pl.pallas_call(
        functools.partial(kernel_body, dims),
        out_shape=results,
        in_specs=[far] * 10,
        out_specs=(anywhere,) * 4,
        scratch_shapes=[
            vm((cells, chans), BF), vm((cells, chans), BF),
            vm((chans, chans), BF), vm((1, chans), F32), vm((chans, chans), BF),
            vm((chans, chans), BF), vm((chans, chans), BF), vm((1, chans), F32),
            vm((1, pipes), jnp.int32), vm((1, pipes), jnp.int32),
            vm((cells // TILE, rows, TILE), BF), vm((cells // TILE, TILE, rows), BF),
            vm((cells, chans), F32), vm((cells, chans), BF), vm((cells, chans), F32),
            vm((cells, chans), BF), vm((cells, chans), BF), vm((rows, chans), F32),
            vm((2, CORES, chips, 2, chans), BF), vm((2, chips, CORES, 2, chans), BF),
            vm((2, chips, CORES, 2, chans), BF), vm((2, chips, CORES, 2, chans), BF),
            vm((2, chips, CORES, 2, chans), BF), vm((2, CORES, chips, 2, chans), BF),
            vm((2, 2, chans), BF), vm((2, line, 2, chans), BF),
            vm((ys, 2 * line, chans), BF), vm((width, ys, 2 * line, chans), BF),
            vm((width, ys, 2 * line, chans), BF),
            vm((ys, line, chans), BF), vm((width, ys, line, chans), BF),
            vm((width, ys, line, chans), BF),
            vm((width, 2, share, chans), F32), vm((width, 2, share, chans), BF),
            vm((width, 2, share, chans), BF), vm((width, 2, share, chans), BF),
            vm((2, chans, chans), F32),
            vm((rows, rows), BF), vm((8, 2 * pipes), BF), vm((8, pipes), BF),
            vm((rows, chans), BF), vm((1, chans), F32), vm((8, chans), F32),
            vm((2 * line, chans), F32),
            pltpu.SemaphoreType.DMA((10,)), pltpu.SemaphoreType.DMA((4,)),
            pltpu.SemaphoreType.DMA((18,)), pltpu.SemaphoreType.DMA((18,)),
        ],
        compiler_params=pltpu.CompilerParams(
            collective_id=0, has_side_effects=True, vmem_limit_bytes=48 << 20
        ),
        name="operator_step",
    )(*(
        pltpu.with_memory_space_constraint(value, pltpu.HBM)
        for value in (
            inputs[0], cotangent[0], point_weight, point_bias[None, :], spec_real[0],
            spec_imag[0], junc_weight, junc_bias[None, :], inlet_ids[None, :],
            outlet_ids[None, :],
        )
    ))
    y, gi, gr, gm = pl.pallas_call(
        deliver,
        out_shape=results,
        in_specs=[pl.BlockSpec(memory_space=pltpu.VMEM)] * 4,
        out_specs=(far,) * 4,
        scratch_shapes=[pltpu.SemaphoreType.DMA((4,))],
        name="deliver",
    )(*(pltpu.with_memory_space_constraint(value, pltpu.VMEM) for value in made))
    return y[None], gi[None], gr[None], gm[None]


def solution(mesh):
    split = P(("len", "pipe"), None, None)
    modes = P("len", None, None)
    return jax.shard_map(
        body,
        mesh=mesh,
        in_specs=(split, split, P(), P(), modes, modes, P(), P(), P(), P()),
        out_specs=(split, split, modes, modes),
        check_vma=False,
    )
```

time: 90.2 us -> 73.1 us (0.81)
  local copies, waits for them, and re-layouts: 10.1 us -> 0 us
  Pallas kernels: 79.1 us -> 72.3 us
    unnamed x24 -> x0, local copies, waits for them, and re-layouts: 10.1 us -> none
    pallas_call x1 -> x2, Pallas kernels: 79.1 us -> 72.3 us  [the longest x1 70.8 us: body(): pl.pallas_call(functools.partial(kernel_body, dims), out_shape=results, i...]
where the time goes in v3:
time: 73.1 us; the launch traced here: 72.9 us
  Pallas kernels  72.3 us (99%)
    pallas_call x1, Pallas kernels, body(): pl.pallas_call(functools.partial(kernel_body, dims), out_shape=results, i...  70.8 us
    pallas_call x1, Pallas kernels, body(): pl.pallas_call(deliver, out_shape=results, in_specs=[pl.BlockSpec(memory_...  1.52 us

profile of v3, /device:TPU:1, one launch (start us, length us, event | category | flops | bytes accessed | tf_op | source)
XLA Modules:
  0.0 72.9 jit_solution(8266066136482877887)
XLA Ops:
  0.6 70.8 %operator_step.1 = (bf16[2048,256]{1,0:T(8,128)(2,1)S(1)}, bf16[2048,256]{1,0:T(8,128)(2,1)S(1)}, f32[256,256]{1,0:T(8,128)S(1)}, f32[256,256]{1,0:T(8,128)S(1)}) custom-call(bf16[2048,256]{1,0:T(8,128)(2,1)} %bitcast.12, bf16[2048,256]{1,0:T(8,128)(2,1)} %bitcast.13, bf16[256,256]{1,0:T(8,128)(2,1)} %pw_hbm.1, f32[1,256]{1,0:T(1,128)} %bitcast.18, ...), custom_call_target="tpu_custom_call" | custom-call | tf_op jit(solution)/shard_map/operator_step/pallas_call | solution.py:472
  71.4 1.5 %deliver.1 = (bf16[2048,256]{1,0:T(8,128)(2,1)}, bf16[2048,256]{1,0:T(8,128)(2,1)}, f32[256,256]{1,0:T(8,128)}, f32[256,256]{1,0:T(8,128)}) custom-call(bf16[2048,256]{1,0:T(8,128)(2,1)S(1)} %get-tuple-element.12.refs_0_, bf16[2048,256]{1,0:T(8,128)(2,1)S(1)} %get-tuple-element.13.refs_1_, f32[256,256]{1,0:T(8,128)S(1)} %get-tuple-element.14.refs_2_, ...), custom_call_target="tpu_custom_call" | custom-call | tf_op jit(solution)/shard_map/deliver/pallas_call | solution.py:514

commit v4 on v3

--- a/solution.py
+++ b/solution.py
@@ -11,6 +11,7 @@
 COUPLING = 0.125
 LINE = 16
 CORES = 2
+FAR = 5
 TILE = 256
 MESH = pl.DeviceIdType.MESH
 BF = jnp.bfloat16
@@ -44,21 +45,16 @@
     return jnp.where(away > quarter, value, -value)
 
 
-def mode_of(row, chips):
-    return (row // 2) % chips * CORES + row // (2 * chips)
-
-
-def base_tables(row, col, cell_count, chips):
-    mode = mode_of(row, chips)
-    index = mode * col + (cell_count // 4) * (row % 2)
+def base_tables(row, col, cell_count):
+    index = row // 2 * col + (cell_count // 4) * (row % 2)
     scale = 1.0 / math.sqrt(cell_count)
     cosine = turn_cos(index % cell_count, cell_count) * scale
     sine = turn_cos((index + 3 * (cell_count // 4)) % cell_count, cell_count) * scale
     return cosine, sine
 
 
-def shift_factors(row, step, steps, chips):
-    index = (mode_of(row, chips) * step) % steps
+def shift_factors(row, step, steps):
+    index = (row // 2 * step) % steps
     return turn_cos(index, steps), turn_cos((index + 3 * (steps // 4)) % steps, steps)
 
 
@@ -68,8 +64,8 @@
     y_out, gi_out, gr_out, gm_out,
     xv, cotv, pw_ref, pb_ref, sr_ref, si_ref, jw_ref, jb_ref, in_ref, out_ref,
     ftab, ttab, pointv, gtv, localv, yv, giv, acc,
-    stage, duo, data, mixd, back, fin,
-    own_z, ag_z, fwd_y, fwd_x, fwd_c, bwd_y, bwd_x, bwd_c,
+    outbox, duo, inbox,
+    own_z, ag_z, fwd_p, fwd_c, bwd_p, bwd_c,
     wfull, wsend, wrecv, wtot, grout,
     perm_q, sel_f, sel_b, scaledv, condv, jactv, rowv,
     load_sem, out_sem, ssem, rsem,
@@ -88,14 +84,19 @@
     def chip_at(dy, dz):
         return (y_me + dy) % ys * line + (z_me + dz) % line
 
-    def on_chip(chip):
-        return {"len": chip * CORES + c_me, "pipe": x_me}
+    def on_chip(chip, core=None):
+        return {"len": chip * CORES + (c_me if core is None else core), "pipe": x_me}
 
     def on_column(k):
         return {"len": len_me, "pipe": (x_me + k) % width}
 
+    def on_plane(dy, k):
+        return {"len": chip_at(dy, 0) * CORES + c_me, "pipe": (x_me + k) % width}
+
     sibling = {"len": chip_me * CORES + c_other, "pipe": x_me}
     y_order = sorted(range(ys), key=lambda k: -min(k, ys - k))
+    x_order = sorted(range(width), key=lambda k: -min(k, width - k))
+    plane = [(dy, k) for dy in y_order for k in x_order][:-1]
 
     def z_step(j):
         return line // 2 + ((j + 1) // 2) * (1 - 2 * (j % 2))
@@ -135,55 +136,57 @@
     def greet(device):
         pl.semaphore_signal(barrier, inc=1, device_id=device, device_id_type=MESH)
 
-    each_chip(lambda chip: greet(on_chip(chip)), 0, line)
-    for k in range(1, width):
-        greet(on_column(k))
+    def greet_both(chip):
+        greet(on_chip(chip))
+        greet(on_chip(chip, c_other))
+
+    each_chip(greet_both, 0, FAR)
+    each_chip(lambda chip: greet(on_chip(chip)), FAR, line)
+    for dy, k in plane:
+        if k:
+            greet(on_plane(dy, k))
     greet(sibling)
 
     row_id = lax.broadcasted_iota(jnp.int32, (rows, TILE), 0)
     col_id = lax.broadcasted_iota(jnp.int32, (rows, TILE), 1)
-    base_cos, base_sin = base_tables(row_id, col_id, cells, chips)
+    base_cos, base_sin = base_tables(row_id, col_id, cells)
     localv[0:rows, :] = base_cos
     localv[rows : 2 * rows, :] = base_sin
     row_one = lax.broadcasted_iota(jnp.int32, (rows, 1), 0)
-    doubled = jnp.where(mode_of(row_one, chips) == 0, 1.0, 2.0)
+    doubled = jnp.where(row_one < 2, 1.0, 2.0)
     acc[...] = jnp.zeros_like(acc)
     loads[0].wait()
 
     def spectra_step(k, carry):
-        turn_c, turn_s = shift_factors(row_one, k, chunks, chips)
+        turn_c, turn_s = shift_factors(row_one, k, chunks)
         table = (localv[0:rows, :] * turn_c - localv[rows : 2 * rows, :] * turn_s).astype(BF)
         ftab[k] = table
         acc[...] += dot(table, xv[pl.ds(k * TILE, TILE), :])
         return carry
 
     lax.fori_loop(0, chunks, spectra_step, 0)
-    stage[0] = acc[...].astype(BF).reshape(CORES, chips, 2, chans)
-    pl.semaphore_wait(barrier, chips - 1 + width - 1 + 1)
-
-    def swap_out(slot, phase):
-        put(phase, stage.at[slot, c_other], duo.at[slot, :, c_me], sibling)
-        duo[slot, :, c_me] = stage[slot, c_me]
-
-    def chips_out(slot, phase, low, high):
-        if low == 0:
-            data[slot, chip_me] = duo[slot, chip_me]
-        each_chip(
-            lambda chip: put(phase, duo.at[slot, chip], data.at[slot, chip_me], on_chip(chip)),
-            low, high,
-        )
-
-    def chips_back(slot, phase, low, high):
-        if low == 0:
-            back[slot, chip_me] = mixd[slot, chip_me]
-        each_chip(
-            lambda chip: put(phase, mixd.at[slot, chip], back.at[slot, chip_me], on_chip(chip)),
-            low, high,
-        )
-
-    def swap_back(slot, phase):
-        put(phase, back.at[slot, :, c_other], fin.at[slot, c_me], sibling)
-        fin[slot, c_me] = back[slot, :, c_me]
+    outbox[0] = acc[...].astype(BF).reshape(chips, CORES, 2, chans)
+    pl.semaphore_wait(barrier, chips - 1 + FAR * ys + ys * (width - 1) + 1)
+
+    def exchange(slot):
+        phase = 2 * slot
+        put(phase, outbox.at[slot, :, c_other], duo.at[slot, :, c_me], sibling)
+        duo[slot, :, c_me] = outbox[slot, :, c_me]
+
+        def direct(chip):
+            for core in (c_me, c_other):
+                put(
+                    phase + 1, outbox.at[slot, chip, core], inbox.at[slot, chip_me, c_me],
+                    on_chip(chip, core),
+                )
+
+        def paired(chip):
+            put(phase + 1, duo.at[slot, chip], inbox.at[slot, chip_me], on_chip(chip))
+
+        each_chip(direct, 0, FAR)
+        drain(rsem, phase, duo.at[slot, :, 0])
+        each_chip(paired, FAR, line)
+        inbox[slot, chip_me] = duo[slot, chip_me]
 
     others = pl.ds(0, chips - 1)
 
@@ -198,32 +201,28 @@
 
         lax.fori_loop(0, line - 1, step, 0)
 
-    def gather_y(ref, phase, block):
-        ref[y_me] = block
-        for dy in y_order[:-1]:
-            put(phase, ref.at[y_me], ref.at[y_me], on_chip(chip_at(dy, 0)))
-
-    def gather_x(source, ref, phase):
-        ref[x_me] = source[...]
-        for k in (2, 1, 3):
-            put(phase, source, ref.at[x_me], on_column(k))
-
-    swap_out(0, 0)
+    def gather_plane(ref, phase, block):
+        here = x_me * ys + y_me
+        ref[here] = block
+        for dy, k in plane:
+            put(phase, ref.at[here], ref.at[here], on_plane(dy, k))
+
+    partners = pl.ds(0, len(plane))
+
     first_row = xv[0:16, :].astype(F32)[0:1, :]
     last_row = xv[cells - 16 : cells, :].astype(F32)[15:16, :]
     gather_z(0, 8, first_row, last_row)
-    drain(rsem, 0, stage.at[0, 0])
-    chips_out(0, 1, 0, line)
+    exchange(0)
 
     cell_id = lax.broadcasted_iota(jnp.int32, (TILE, rows), 0)
     mode_id = lax.broadcasted_iota(jnp.int32, (TILE, rows), 1)
-    side_cos, side_sin = base_tables(mode_id, cell_id, cells, chips)
+    side_cos, side_sin = base_tables(mode_id, cell_id, cells)
     localv[0:TILE, :] = side_cos
     localv[TILE : 2 * TILE, :] = side_sin
     col_one = lax.broadcasted_iota(jnp.int32, (1, rows), 1)
 
     def side_step(k, carry):
-        turn_c, turn_s = shift_factors(col_one, k, chunks, chips)
+        turn_c, turn_s = shift_factors(col_one, k, chunks)
         ttab[k] = (localv[0:TILE, :] * turn_c - localv[TILE : 2 * TILE, :] * turn_s).astype(BF)
         return carry
 
@@ -240,17 +239,16 @@
     drain(rsem, 8, ag_z.at[0, pl.ds(0, line - 1)])
     for spot in range(line):
         rowv[2 * spot : 2 * spot + 2, :] = ag_z[0, spot].astype(F32)
-    gather_y(fwd_y, 9, rowv[...].astype(BF))
-
-    drain(rsem, 1, data.at[0, others])
-    seen = data[0].reshape(rows, chans)
+    gather_plane(fwd_p, 9, rowv[...].astype(BF))
+
+    drain(rsem, 1, inbox.at[0, others])
+    seen = inbox[0].reshape(rows, chans)
     turned = dot(perm_q[...], seen).astype(BF)
     mixed = dot(seen, sr_ref[...]) + dot(turned, si_ref[...])
-    mixd[0] = mixed.astype(BF).reshape(chips, CORES, 2, chans)
-    chips_back(0, 2, 0, line)
-
-    drain(rsem, 9, fwd_y.at[pl.ds(0, ys - 1)])
-    gather_x(fwd_y, fwd_x, 10)
+    outbox[1] = mixed.astype(BF).reshape(chips, CORES, 2, chans)
+    exchange(1)
+    drain(rsem, 9, fwd_p.at[partners])
+    put(10, fwd_p, fwd_c, sibling)
 
     ids_in, ids_out = in_ref[...].astype(F32), out_ref[...].astype(F32)
     place = lax.broadcasted_iota(jnp.int32, (1, pipes), 1)
@@ -288,13 +286,8 @@
 
     lax.fori_loop(0, chunks, point_step, 0)
 
-    drain(rsem, 10, fwd_x.at[pl.ds(0, width - 1)])
-    put(11, fwd_x, fwd_c, sibling)
-    drain(rsem, 2, back.at[0, others])
-    swap_back(0, 3)
-
-    drain(rsem, 11, fwd_c)
-    sums = dot(sel_f[:, 0:pipes], fwd_x[...].reshape(pipes, chans)) + dot(
+    drain(rsem, 10, fwd_c)
+    sums = dot(sel_f[:, 0:pipes], fwd_p[...].reshape(pipes, chans)) + dot(
         sel_f[:, pipes : 2 * pipes], fwd_c[...].reshape(pipes, chans)
     )
     junc_act = dot(sums.astype(BF), jw_ref[...]) + jb_ref[...]
@@ -303,8 +296,8 @@
     condv[...] = COUPLING * (junc_rows[0:1, :] + junc_rows[1:2, :])
     loads[9].wait()
 
-    drain(rsem, 3, fin.at[0, 0])
-    scaledv[...] = (fin[0].reshape(rows, chans).astype(F32) * doubled).astype(BF)
+    drain(rsem, 3, inbox.at[1, others])
+    scaledv[...] = (inbox[1].reshape(rows, chans).astype(F32) * doubled).astype(BF)
 
     acc[...] = jnp.zeros_like(acc)
 
@@ -323,13 +316,11 @@
         acc[...] += dot(ftab[k], grad)
         return total + jnp.sum(grad.astype(F32), axis=0, keepdims=True)
 
-    grad_cond = lax.fori_loop(0, chunks, gelu_step, jnp.zeros((1, chans), F32))
-    stage[1] = (acc[...] * doubled).astype(BF).reshape(CORES, chips, 2, chans)
-    swap_out(1, 4)
+    grad_cond = lax.fori_loop(0, chunks, gelu_step, jnp.zeros((1, chans), F32), unroll=True)
+    outbox[2] = (acc[...] * doubled).astype(BF).reshape(chips, CORES, 2, chans)
     high = grad_cond.astype(BF).astype(F32)
-    gather_z(1, 12, high, grad_cond - high)
-    drain(rsem, 4, stage.at[0, 0])
-    chips_out(1, 5, 0, line)
+    gather_z(1, 11, high, grad_cond - high)
+    exchange(2)
     put_y = pltpu.make_async_copy(yv, y_out, out_sem.at[0])
     put_y.start()
 
@@ -340,17 +331,17 @@
 
     lax.fori_loop(0, chunks, local_step, 0)
 
-    drain(rsem, 12, ag_z.at[1, pl.ds(0, line - 1)])
+    drain(rsem, 11, ag_z.at[1, pl.ds(0, line - 1)])
     for spot in range(line):
         rowv[spot : spot + 1, :] = jnp.sum(ag_z[1, spot].astype(F32), axis=0, keepdims=True)
-    gather_y(bwd_y, 13, rowv[0:line, :].astype(BF))
-
-    drain(rsem, 5, data.at[1, others])
-    grads = data[1].reshape(rows, chans)
+    gather_plane(bwd_p, 12, rowv[0:line, :].astype(BF))
+
+    drain(rsem, 5, inbox.at[2, others])
+    grads = inbox[2].reshape(rows, chans)
     flipped = dot_tn(perm_q[...], grads).astype(BF)
     returned = dot_nt(grads, sr_ref[...]) + dot_nt(flipped, si_ref[...])
-    mixd[1] = returned.astype(BF).reshape(chips, CORES, 2, chans)
-    seen = data[0].reshape(rows, chans)
+    outbox[3] = returned.astype(BF).reshape(chips, CORES, 2, chans)
+    seen = inbox[0].reshape(rows, chans)
     real = dot_tn(seen, grads)
     imag = dot_tn(seen, flipped)
     share = chans // width
@@ -359,28 +350,25 @@
         wfull[column, 0] = real[cut, :]
         wfull[column, 1] = imag[cut, :]
     wsend[...] = wfull[...].astype(BF)
-    for k in (2, 1, 3):
-        put(16, wsend.at[(x_me + k) % width], wrecv.at[x_me], on_column(k))
-    chips_back(1, 6, 0, line // 2)
-    drain(rsem, 13, bwd_y.at[pl.ds(0, ys - 1)])
-    gather_x(bwd_y, bwd_x, 14)
-    chips_back(1, 6, line // 2, line)
-
-    drain(rsem, 16, wrecv.at[pl.ds(0, width - 1)])
+    for k in x_order[:-1]:
+        put(14, wsend.at[(x_me + k) % width], wrecv.at[x_me], on_column(k))
+    exchange(3)
+    drain(rsem, 12, bwd_p.at[partners])
+    put(13, bwd_p, bwd_c, sibling)
+
+    drain(rsem, 14, wrecv.at[pl.ds(0, width - 1)])
     wrecv[x_me] = jnp.zeros(wrecv.shape[1:], BF)
     total = wfull[x_me]
     for column in range(width):
         total = total + wrecv[column].astype(F32)
     wtot[x_me] = total.astype(BF)
-    for k in (2, 1, 3):
-        put(17, wtot.at[x_me], wtot.at[x_me], on_column(k))
-
-    drain(rsem, 14, bwd_x.at[pl.ds(0, width - 1)])
-    put(15, bwd_x, bwd_c, sibling)
-    drain(rsem, 15, bwd_c)
+    for k in x_order[:-1]:
+        put(15, wtot.at[x_me], wtot.at[x_me], on_column(k))
+
+    drain(rsem, 13, bwd_c)
     half_pipes = pipes // 2
     junc_grad = COUPLING * (
-        dot(sel_b[:, 0:half_pipes], bwd_x[...].reshape(half_pipes, chans))
+        dot(sel_b[:, 0:half_pipes], bwd_p[...].reshape(half_pipes, chans))
         + dot(sel_b[:, half_pipes:pipes], bwd_c[...].reshape(half_pipes, chans))
     )
     junc_act = jactv[...]
@@ -388,13 +376,11 @@
     act_grad = (junc_grad * (gate * (1.0 + junc_act * (1.0 - gate)))).astype(BF)
     jactv[...] = dot_nt(act_grad, jw_ref[...]).astype(BF).astype(F32)
 
-    drain(rsem, 6, back.at[1, others])
-    swap_back(1, 7)
-    drain(rsem, 7, fin.at[1, 0])
+    drain(rsem, 7, inbox.at[3, others])
 
     def final_step(k, ends):
         part_rows = pl.ds(k * TILE, TILE)
-        spread = dot(ttab[k], fin[1].reshape(rows, chans))
+        spread = dot(ttab[k], inbox[3].reshape(rows, chans))
         if ends is not None:
             spread = spread + ends
         giv[part_rows, :] = (localv[part_rows, :] + spread.astype(BF).astype(F32)).astype(BF)
@@ -407,10 +393,10 @@
         final_step(k, None)
         return carry
 
-    lax.fori_loop(1, chunks - 1, final_loop, 0)
+    lax.fori_loop(1, chunks - 1, final_loop, 0, unroll=True)
     final_step(chunks - 1, jnp.where(tile_row == TILE - 1, jactv[1:2, :], 0.0))
 
-    drain(rsem, 17, wtot.at[pl.ds(0, width - 1)])
+    drain(rsem, 15, wtot.at[pl.ds(0, width - 1)])
     for column in range(width):
         cut = slice(column * share, (column + 1) * share)
         grout[0, cut, :] = wtot[column, 0].astype(F32)
@@ -420,14 +406,15 @@
     put_real.start()
     put_imag.start()
 
+    for slot in range(4):
+        drain(ssem, 2 * slot, duo.at[slot, :, 0])
+        drain(ssem, 2 * slot + 1, inbox.at[slot, others])
     for phase, part in (
-        (0, stage.at[0, 0]), (1, data.at[0, others]), (2, back.at[0, others]), (3, fin.at[0, 0]),
-        (4, stage.at[0, 0]), (5, data.at[1, others]), (6, back.at[1, others]), (7, fin.at[1, 0]),
-        (8, ag_z.at[0, pl.ds(0, line - 1)]), (9, fwd_y.at[pl.ds(0, ys - 1)]),
-        (10, fwd_x.at[pl.ds(0, width - 1)]), (11, fwd_c),
-        (12, ag_z.at[1, pl.ds(0, line - 1)]), (13, bwd_y.at[pl.ds(0, ys - 1)]),
-        (14, bwd_x.at[pl.ds(0, width - 1)]), (15, bwd_c),
-        (16, wrecv.at[pl.ds(0, width - 1)]), (17, wtot.at[pl.ds(0, width - 1)]),
+        (8, ag_z.at[0, pl.ds(0, line - 1)]),
+        (9, fwd_p.at[partners]), (10, fwd_c),
+        (11, ag_z.at[1, pl.ds(0, line - 1)]),
+        (12, bwd_p.at[partners]), (13, bwd_c),
+        (14, wrecv.at[pl.ds(0, width - 1)]), (15, wtot.at[pl.ds(0, width - 1)]),
     ):
         drain(ssem, phase, part)
     put_y.wait()
@@ -482,14 +469,11 @@
             vm((cells // TILE, rows, TILE), BF), vm((cells // TILE, TILE, rows), BF),
             vm((cells, chans), F32), vm((cells, chans), BF), vm((cells, chans), F32),
             vm((cells, chans), BF), vm((cells, chans), BF), vm((rows, chans), F32),
-            vm((2, CORES, chips, 2, chans), BF), vm((2, chips, CORES, 2, chans), BF),
-            vm((2, chips, CORES, 2, chans), BF), vm((2, chips, CORES, 2, chans), BF),
-            vm((2, chips, CORES, 2, chans), BF), vm((2, CORES, chips, 2, chans), BF),
+            vm((4, chips, CORES, 2, chans), BF), vm((4, chips, CORES, 2, chans), BF),
+            vm((4, chips, CORES, 2, chans), BF),
             vm((2, 2, chans), BF), vm((2, line, 2, chans), BF),
-            vm((ys, 2 * line, chans), BF), vm((width, ys, 2 * line, chans), BF),
-            vm((width, ys, 2 * line, chans), BF),
-            vm((ys, line, chans), BF), vm((width, ys, line, chans), BF),
-            vm((width, ys, line, chans), BF),
+            vm((width * ys, 2 * line, chans), BF), vm((width * ys, 2 * line, chans), BF),
+            vm((width * ys, line, chans), BF), vm((width * ys, line, chans), BF),
             vm((width, 2, share, chans), F32), vm((width, 2, share, chans), BF),
             vm((width, 2, share, chans), BF), vm((width, 2, share, chans), BF),
             vm((2, chans, chans), F32),
@@ -497,7 +481,7 @@
             vm((rows, chans), BF), vm((1, chans), F32), vm((8, chans), F32),
             vm((2 * line, chans), F32),
             pltpu.SemaphoreType.DMA((10,)), pltpu.SemaphoreType.DMA((4,)),
-            pltpu.SemaphoreType.DMA((18,)), pltpu.SemaphoreType.DMA((18,)),
+            pltpu.SemaphoreType.DMA((16,)), pltpu.SemaphoreType.DMA((16,)),
         ],
         compiler_params=pltpu.CompilerParams(
             collective_id=0, has_side_effects=True, vmem_limit_bytes=48 << 20

time: 73.1 us -> 68.4 us (0.936)
  Pallas kernels: 72.3 us -> 67.5 us
    pallas_call x1, Pallas kernels: 70.8 us -> 65.9 us  [body(): pl.pallas_call(functools.partial(kernel_body, dims), out_shape=results, i...]
where the time goes in v4:
time: 68.4 us; the launch traced here: 68.1 us
  Pallas kernels  67.5 us (99%)
    pallas_call x1, Pallas kernels, body(): pl.pallas_call(functools.partial(kernel_body, dims), out_shape=results, i...  65.9 us
    pallas_call x1, Pallas kernels, body(): pl.pallas_call(deliver, out_shape=results, in_specs=[pl.BlockSpec(memory_...  1.52 us

profile of v4, /device:TPU:1, one launch (start us, length us, event | category | flops | bytes accessed | tf_op | source)
XLA Modules:
  0.0 68.1 jit_solution(10759136885262353899)
XLA Ops:
  0.6 65.9 %operator_step.1 = (bf16[2048,256]{1,0:T(8,128)(2,1)S(1)}, bf16[2048,256]{1,0:T(8,128)(2,1)S(1)}, f32[256,256]{1,0:T(8,128)S(1)}, f32[256,256]{1,0:T(8,128)S(1)}) custom-call(bf16[2048,256]{1,0:T(8,128)(2,1)} %bitcast.12, bf16[2048,256]{1,0:T(8,128)(2,1)} %bitcast.13, bf16[256,256]{1,0:T(8,128)(2,1)} %pw_hbm.1, f32[1,256]{1,0:T(1,128)} %bitcast.18, ...), custom_call_target="tpu_custom_call" | custom-call | tf_op jit(solution)/shard_map/operator_step/pallas_call | solution.py:459
  66.6 1.5 %deliver.1 = (bf16[2048,256]{1,0:T(8,128)(2,1)}, bf16[2048,256]{1,0:T(8,128)(2,1)}, f32[256,256]{1,0:T(8,128)}, f32[256,256]{1,0:T(8,128)}) custom-call(bf16[2048,256]{1,0:T(8,128)(2,1)S(1)} %get-tuple-element.12.refs_0_, bf16[2048,256]{1,0:T(8,128)(2,1)S(1)} %get-tuple-element.13.refs_1_, f32[256,256]{1,0:T(8,128)S(1)} %get-tuple-element.14.refs_2_, ...), custom_call_target="tpu_custom_call" | custom-call | tf_op jit(solution)/shard_map/deliver/pallas_call | solution.py:498

commit v5 on v4

--- a/solution.py
+++ b/solution.py
@@ -61,14 +61,14 @@
 def kernel_body(
     dims,
     x_hbm, cot_hbm, pw_hbm, pb_hbm, sr_hbm, si_hbm, jw_hbm, jb_hbm, in_hbm, out_hbm,
-    y_out, gi_out, gr_out, gm_out,
+    yv, localv, ttab, modes, jactv, grv, gmv,
     xv, cotv, pw_ref, pb_ref, sr_ref, si_ref, jw_ref, jb_ref, in_ref, out_ref,
-    ftab, ttab, pointv, gtv, localv, yv, giv, acc,
+    ftab, pointv, gtv, acc,
     outbox, duo, inbox,
     own_z, ag_z, fwd_p, fwd_c, bwd_p, bwd_c,
-    wfull, wsend, wrecv, wtot, grout,
-    perm_q, sel_f, sel_b, scaledv, condv, jactv, rowv,
-    load_sem, out_sem, ssem, rsem,
+    wfull, wsend, wrecv, wtot,
+    perm_q, sel_f, sel_b, scaledv, condv, rowv,
+    load_sem, ssem, rsem,
 ):
     line, ys, width, pipes = dims["line"], dims["ys"], dims["width"], dims["pipes"]
     cells, chans, rows = dims["cells"], dims["chans"], dims["rows"]
@@ -121,6 +121,22 @@
             for dy in y_order[:-1]:
                 action(chip_at(dy, 0))
 
+    barrier = pltpu.get_barrier_semaphore()
+
+    def greet(device):
+        pl.semaphore_signal(barrier, inc=1, device_id=device, device_id_type=MESH)
+
+    def greet_both(chip):
+        greet(on_chip(chip))
+        greet(on_chip(chip, c_other))
+
+    each_chip(greet_both, 0, FAR)
+    each_chip(lambda chip: greet(on_chip(chip)), FAR, line)
+    for dy, k in plane:
+        if k:
+            greet(on_plane(dy, k))
+    greet(sibling)
+
     loads = [
         pltpu.make_async_copy(source, target, load_sem.at[i])
         for i, (source, target) in enumerate((
@@ -131,22 +147,6 @@
     for load in loads:
         load.start()
 
-    barrier = pltpu.get_barrier_semaphore()
-
-    def greet(device):
-        pl.semaphore_signal(barrier, inc=1, device_id=device, device_id_type=MESH)
-
-    def greet_both(chip):
-        greet(on_chip(chip))
-        greet(on_chip(chip, c_other))
-
-    each_chip(greet_both, 0, FAR)
-    each_chip(lambda chip: greet(on_chip(chip)), FAR, line)
-    for dy, k in plane:
-        if k:
-            greet(on_plane(dy, k))
-    greet(sibling)
-
     row_id = lax.broadcasted_iota(jnp.int32, (rows, TILE), 0)
     col_id = lax.broadcasted_iota(jnp.int32, (rows, TILE), 1)
     base_cos, base_sin = base_tables(row_id, col_id, cells)
@@ -166,6 +166,25 @@
 
     lax.fori_loop(0, chunks, spectra_step, 0)
     outbox[0] = acc[...].astype(BF).reshape(chips, CORES, 2, chans)
+    cell_id = lax.broadcasted_iota(jnp.int32, (TILE, rows), 0)
+    mode_id = lax.broadcasted_iota(jnp.int32, (TILE, rows), 1)
+    side_cos, side_sin = base_tables(mode_id, cell_id, cells)
+    localv[0:TILE, :] = side_cos
+    localv[TILE : 2 * TILE, :] = side_sin
+    col_one = lax.broadcasted_iota(jnp.int32, (1, rows), 1)
+
+    def side_step(k, carry):
+        turn_c, turn_s = shift_factors(col_one, k, chunks)
+        ttab[k] = (localv[0:TILE, :] * turn_c - localv[TILE : 2 * TILE, :] * turn_s).astype(BF)
+        return carry
+
+    lax.fori_loop(0, chunks, side_step, 0)
+
+    to_row = lax.broadcasted_iota(jnp.int32, (rows, rows), 0)
+    from_row = lax.broadcasted_iota(jnp.int32, (rows, rows), 1)
+    swapped = jnp.where(to_row % 2 == 0, to_row + 1, to_row - 1)
+    sign = jnp.where(to_row % 2 == 0, -1.0, 1.0)
+    perm_q[...] = jnp.where(from_row == swapped, sign, 0.0).astype(BF)
     pl.semaphore_wait(barrier, chips - 1 + FAR * ys + ys * (width - 1) + 1)
 
     def exchange(slot):
@@ -214,41 +233,8 @@
     gather_z(0, 8, first_row, last_row)
     exchange(0)
 
-    cell_id = lax.broadcasted_iota(jnp.int32, (TILE, rows), 0)
-    mode_id = lax.broadcasted_iota(jnp.int32, (TILE, rows), 1)
-    side_cos, side_sin = base_tables(mode_id, cell_id, cells)
-    localv[0:TILE, :] = side_cos
-    localv[TILE : 2 * TILE, :] = side_sin
-    col_one = lax.broadcasted_iota(jnp.int32, (1, rows), 1)
-
-    def side_step(k, carry):
-        turn_c, turn_s = shift_factors(col_one, k, chunks)
-        ttab[k] = (localv[0:TILE, :] * turn_c - localv[TILE : 2 * TILE, :] * turn_s).astype(BF)
-        return carry
-
-    lax.fori_loop(0, chunks, side_step, 0)
-
-    to_row = lax.broadcasted_iota(jnp.int32, (rows, rows), 0)
-    from_row = lax.broadcasted_iota(jnp.int32, (rows, rows), 1)
-    swapped = jnp.where(to_row % 2 == 0, to_row + 1, to_row - 1)
-    sign = jnp.where(to_row % 2 == 0, -1.0, 1.0)
-    perm_q[...] = jnp.where(from_row == swapped, sign, 0.0).astype(BF)
     for load in loads[1:9]:
         load.wait()
-
-    drain(rsem, 8, ag_z.at[0, pl.ds(0, line - 1)])
-    for spot in range(line):
-        rowv[2 * spot : 2 * spot + 2, :] = ag_z[0, spot].astype(F32)
-    gather_plane(fwd_p, 9, rowv[...].astype(BF))
-
-    drain(rsem, 1, inbox.at[0, others])
-    seen = inbox[0].reshape(rows, chans)
-    turned = dot(perm_q[...], seen).astype(BF)
-    mixed = dot(seen, sr_ref[...]) + dot(turned, si_ref[...])
-    outbox[1] = mixed.astype(BF).reshape(chips, CORES, 2, chans)
-    exchange(1)
-    drain(rsem, 9, fwd_p.at[partners])
-    put(10, fwd_p, fwd_c, sibling)
 
     ids_in, ids_out = in_ref[...].astype(F32), out_ref[...].astype(F32)
     place = lax.broadcasted_iota(jnp.int32, (1, pipes), 1)
@@ -278,6 +264,20 @@
     pipe_row = lax.broadcasted_iota(jnp.int32, (pipes, pipes), 0)
     hot = jnp.where(pipe_row == pipe_of(entry), 1.0, 0.0).astype(BF)
     sel_b[...] = (dot(match_in, hot) + dot(match_out, hot)).astype(BF)
+
+    drain(rsem, 8, ag_z.at[0, pl.ds(0, line - 1)])
+    for spot in range(line):
+        rowv[2 * spot : 2 * spot + 2, :] = ag_z[0, spot].astype(F32)
+    gather_plane(fwd_p, 9, rowv[...].astype(BF))
+
+    drain(rsem, 1, inbox.at[0, others])
+    seen = inbox[0].reshape(rows, chans)
+    turned = dot(perm_q[...], seen).astype(BF)
+    mixed = dot(seen, sr_ref[...]) + dot(turned, si_ref[...])
+    outbox[1] = mixed.astype(BF).reshape(chips, CORES, 2, chans)
+    exchange(1)
+    drain(rsem, 9, fwd_p.at[partners])
+    put(10, fwd_p, fwd_c, sibling)
 
     def point_step(k, carry):
         part_rows = pl.ds(k * TILE, TILE)
@@ -321,9 +321,6 @@
     high = grad_cond.astype(BF).astype(F32)
     gather_z(1, 11, high, grad_cond - high)
     exchange(2)
-    put_y = pltpu.make_async_copy(yv, y_out, out_sem.at[0])
-    put_y.start()
-
     def local_step(k, carry):
         part_rows = pl.ds(k * TILE, TILE)
         localv[part_rows, :] = dot_nt(gtv[part_rows, :], pw_ref[...])
@@ -377,35 +374,13 @@
     jactv[...] = dot_nt(act_grad, jw_ref[...]).astype(BF).astype(F32)
 
     drain(rsem, 7, inbox.at[3, others])
-
-    def final_step(k, ends):
-        part_rows = pl.ds(k * TILE, TILE)
-        spread = dot(ttab[k], inbox[3].reshape(rows, chans))
-        if ends is not None:
-            spread = spread + ends
-        giv[part_rows, :] = (localv[part_rows, :] + spread.astype(BF).astype(F32)).astype(BF)
-        pltpu.make_async_copy(giv.at[part_rows], gi_out.at[part_rows], out_sem.at[3]).start()
-
-    tile_row = lax.broadcasted_iota(jnp.int32, (TILE, chans), 0)
-    final_step(0, jnp.where(tile_row == 0, jactv[0:1, :], 0.0))
-
-    def final_loop(k, carry):
-        final_step(k, None)
-        return carry
-
-    lax.fori_loop(1, chunks - 1, final_loop, 0, unroll=True)
-    final_step(chunks - 1, jnp.where(tile_row == TILE - 1, jactv[1:2, :], 0.0))
+    modes[...] = inbox[3].reshape(rows, chans)
 
     drain(rsem, 15, wtot.at[pl.ds(0, width - 1)])
     for column in range(width):
         cut = slice(column * share, (column + 1) * share)
-        grout[0, cut, :] = wtot[column, 0].astype(F32)
-        grout[1, cut, :] = wtot[column, 1].astype(F32)
-    put_real = pltpu.make_async_copy(grout.at[0], gr_out, out_sem.at[1])
-    put_imag = pltpu.make_async_copy(grout.at[1], gm_out, out_sem.at[2])
-    put_real.start()
-    put_imag.start()
-
+        grv[cut, :] = wtot[column, 0].astype(F32)
+        gmv[cut, :] = wtot[column, 1].astype(F32)
     for slot in range(4):
         drain(ssem, 2 * slot, duo.at[slot, :, 0])
         drain(ssem, 2 * slot + 1, inbox.at[slot, others])
@@ -417,19 +392,33 @@
         (14, wrecv.at[pl.ds(0, width - 1)]), (15, wtot.at[pl.ds(0, width - 1)]),
     ):
         drain(ssem, phase, part)
-    put_y.wait()
-    put_real.wait()
-    put_imag.wait()
-    pltpu.make_async_copy(giv, gi_out, out_sem.at[3]).wait()
-
-
-def deliver(*refs):
-    count = (len(refs) - 1) // 2
+
+
+def deliver(
+    y_ref, local_ref, tab_ref, modes_ref, ends_ref, gr_ref, gm_ref,
+    y_out, gi_out, gr_out, gm_out, giv, sems,
+):
     copies = [
-        pltpu.make_async_copy(refs[i], refs[count + i], refs[-1].at[i]) for i in range(count)
+        pltpu.make_async_copy(source, target, sems.at[i])
+        for i, (source, target) in enumerate(
+            ((y_ref, y_out), (gr_ref, gr_out), (gm_ref, gm_out))
+        )
     ]
     for copy in copies:
         copy.start()
+    chunks = tab_ref.shape[0]
+    tile_row = lax.broadcasted_iota(jnp.int32, (TILE, giv.shape[1]), 0)
+    for k in range(chunks):
+        part_rows = pl.ds(k * TILE, TILE)
+        spread = dot(tab_ref[k], modes_ref[...])
+        if k == 0:
+            spread = spread + jnp.where(tile_row == 0, ends_ref[0:1, :], 0.0)
+        if k == chunks - 1:
+            spread = spread + jnp.where(tile_row == TILE - 1, ends_ref[1:2, :], 0.0)
+        giv[part_rows, :] = (local_ref[part_rows, :] + spread.astype(BF).astype(F32)).astype(BF)
+        copy = pltpu.make_async_copy(giv.at[part_rows], gi_out.at[part_rows], sems.at[3 + k])
+        copy.start()
+        copies.append(copy)
     for copy in copies:
         copy.wait()
 
@@ -449,26 +438,31 @@
     share = chans // width
     vm = pltpu.VMEM
     far = pl.BlockSpec(memory_space=pltpu.HBM)
-    anywhere = pl.BlockSpec(memory_space=pl.ANY)
+    near = pl.BlockSpec(memory_space=pltpu.VMEM)
     results = (
         jax.ShapeDtypeStruct((cells, chans), BF),
         jax.ShapeDtypeStruct((cells, chans), BF),
         jax.ShapeDtypeStruct((chans, chans), F32),
         jax.ShapeDtypeStruct((chans, chans), F32),
     )
+    chunks = cells // TILE
     made = pl.pallas_call(
         functools.partial(kernel_body, dims),
-        out_shape=results,
+        out_shape=(
+            results[0], jax.ShapeDtypeStruct((cells, chans), F32),
+            jax.ShapeDtypeStruct((chunks, TILE, rows), BF),
+            jax.ShapeDtypeStruct((rows, chans), BF), jax.ShapeDtypeStruct((8, chans), F32),
+            results[2], results[3],
+        ),
         in_specs=[far] * 10,
-        out_specs=(anywhere,) * 4,
+        out_specs=(near,) * 7,
         scratch_shapes=[
             vm((cells, chans), BF), vm((cells, chans), BF),
             vm((chans, chans), BF), vm((1, chans), F32), vm((chans, chans), BF),
             vm((chans, chans), BF), vm((chans, chans), BF), vm((1, chans), F32),
             vm((1, pipes), jnp.int32), vm((1, pipes), jnp.int32),
-            vm((cells // TILE, rows, TILE), BF), vm((cells // TILE, TILE, rows), BF),
-            vm((cells, chans), F32), vm((cells, chans), BF), vm((cells, chans), F32),
-            vm((cells, chans), BF), vm((cells, chans), BF), vm((rows, chans), F32),
+            vm((chunks, rows, TILE), BF), vm((cells, chans), F32), vm((cells, chans), BF),
+            vm((rows, chans), F32),
             vm((4, chips, CORES, 2, chans), BF), vm((4, chips, CORES, 2, chans), BF),
             vm((4, chips, CORES, 2, chans), BF),
             vm((2, 2, chans), BF), vm((2, line, 2, chans), BF),
@@ -476,11 +470,10 @@
             vm((width * ys, line, chans), BF), vm((width * ys, line, chans), BF),
             vm((width, 2, share, chans), F32), vm((width, 2, share, chans), BF),
             vm((width, 2, share, chans), BF), vm((width, 2, share, chans), BF),
-            vm((2, chans, chans), F32),
             vm((rows, rows), BF), vm((8, 2 * pipes), BF), vm((8, pipes), BF),
-            vm((rows, chans), BF), vm((1, chans), F32), vm((8, chans), F32),
+            vm((rows, chans), BF), vm((1, chans), F32),
             vm((2 * line, chans), F32),
-            pltpu.SemaphoreType.DMA((10,)), pltpu.SemaphoreType.DMA((4,)),
+            pltpu.SemaphoreType.DMA((10,)),
             pltpu.SemaphoreType.DMA((16,)), pltpu.SemaphoreType.DMA((16,)),
         ],
         compiler_params=pltpu.CompilerParams(
@@ -498,9 +491,10 @@
     y, gi, gr, gm = pl.pallas_call(
         deliver,
         out_shape=results,
-        in_specs=[pl.BlockSpec(memory_space=pltpu.VMEM)] * 4,
+        in_specs=[near] * 7,
         out_specs=(far,) * 4,
-        scratch_shapes=[pltpu.SemaphoreType.DMA((4,))],
+        scratch_shapes=[vm((cells, chans), BF), pltpu.SemaphoreType.DMA((3 + chunks,))],
+        compiler_params=pltpu.CompilerParams(vmem_limit_bytes=16 << 20),
         name="deliver",
     )(*(pltpu.with_memory_space_constraint(value, pltpu.VMEM) for value in made))
     return y[None], gi[None], gr[None], gm[None]

time: 68.4 us -> 65.9 us (0.963)
  Pallas kernels: 67.5 us -> 65.1 us
    pallas_call x2, Pallas kernels: 67.5 us -> 65.1 us  [the longest x1 63.6 us: body(): pl.pallas_call(functools.partial(kernel_body, dims), out_shape=(results[0...]
where the time goes in v5:
time: 65.9 us; the launch traced here: 65.8 us
  Pallas kernels  65.1 us (99%)
    pallas_call x1, Pallas kernels, body(): pl.pallas_call(functools.partial(kernel_body, dims), out_shape=(results[0...  63.6 us
    pallas_call x1, Pallas kernels, body(): pl.pallas_call(deliver, out_shape=results, in_specs=[near] * 7, out_specs...  1.58 us

profile of v5, /device:TPU:1, one launch (start us, length us, event | category | flops | bytes accessed | tf_op | source)
XLA Modules:
  0.0 65.8 jit_solution(12047836686070864638)
XLA Ops:
  0.6 63.6 %operator_step.1 = (bf16[2048,256]{1,0:T(8,128)(2,1)S(1)}, f32[2048,256]{1,0:T(8,128)S(1)}, bf16[8,256,256]{2,1,0:T(8,128)(2,1)S(1)}, bf16[256,256]{1,0:T(8,128)...) custom-call(bf16[2048,256]{1,0:T(8,128)(2,1)} %bitcast.12, ...), custom_call_target="tpu_custom_call" | custom-call | tf_op jit(solution)/shard_map/operator_step/pallas_call | solution.py:449
  64.2 1.6 %deliver.1 = (bf16[2048,256]{1,0:T(8,128)(2,1)}, bf16[2048,256]{1,0:T(8,128)(2,1)}, f32[256,256]{1,0:T(8,128)}, f32[256,256]{1,0:T(8,128)}) custom-call(bf16[2048,256]{1,0:T(8,128)(2,1)S(1)} %get-tuple-element.15.y_ref, f32[2048,256]{1,0:T(8,128)S(1)} %get-tuple-element.16.local_ref, bf16[8,256,256]{2,1,0:T(8,128)(2,1)S(1)} %get-tuple-element.17.tab_ref, ...), custom_call_target="tpu_custom_call" | custom-call | tf_op jit(solution)/shard_map/deliver/pallas_call | solution.py:491

commit v6 on v5

--- a/solution.py
+++ b/solution.py
@@ -187,10 +187,9 @@
     perm_q[...] = jnp.where(from_row == swapped, sign, 0.0).astype(BF)
     pl.semaphore_wait(barrier, chips - 1 + FAR * ys + ys * (width - 1) + 1)
 
-    def exchange(slot):
+    def exchange(slot, between=None):
         phase = 2 * slot
         put(phase, outbox.at[slot, :, c_other], duo.at[slot, :, c_me], sibling)
-        duo[slot, :, c_me] = outbox[slot, :, c_me]
 
         def direct(chip):
             for core in (c_me, c_other):
@@ -203,6 +202,9 @@
             put(phase + 1, duo.at[slot, chip], inbox.at[slot, chip_me], on_chip(chip))
 
         each_chip(direct, 0, FAR)
+        duo[slot, :, c_me] = outbox[slot, :, c_me]
+        if between is not None:
+            between()
         drain(rsem, phase, duo.at[slot, :, 0])
         each_chip(paired, FAR, line)
         inbox[slot, chip_me] = duo[slot, chip_me]
@@ -230,8 +232,7 @@
 
     first_row = xv[0:16, :].astype(F32)[0:1, :]
     last_row = xv[cells - 16 : cells, :].astype(F32)[15:16, :]
-    gather_z(0, 8, first_row, last_row)
-    exchange(0)
+    exchange(0, lambda: gather_z(0, 8, first_row, last_row))
 
     for load in loads[1:9]:
         load.wait()
@@ -338,18 +339,21 @@
     flipped = dot_tn(perm_q[...], grads).astype(BF)
     returned = dot_nt(grads, sr_ref[...]) + dot_nt(flipped, si_ref[...])
     outbox[3] = returned.astype(BF).reshape(chips, CORES, 2, chans)
-    seen = inbox[0].reshape(rows, chans)
-    real = dot_tn(seen, grads)
-    imag = dot_tn(seen, flipped)
     share = chans // width
-    for column in range(width):
-        cut = slice(column * share, (column + 1) * share)
-        wfull[column, 0] = real[cut, :]
-        wfull[column, 1] = imag[cut, :]
-    wsend[...] = wfull[...].astype(BF)
-    for k in x_order[:-1]:
-        put(14, wsend.at[(x_me + k) % width], wrecv.at[x_me], on_column(k))
-    exchange(3)
+
+    def weight_terms():
+        seen = inbox[0].reshape(rows, chans)
+        real = dot_tn(seen, grads)
+        imag = dot_tn(seen, flipped)
+        for column in range(width):
+            cut = slice(column * share, (column + 1) * share)
+            wfull[column, 0] = real[cut, :]
+            wfull[column, 1] = imag[cut, :]
+        wsend[...] = wfull[...].astype(BF)
+        for k in x_order[:-1]:
+            put(14, wsend.at[(x_me + k) % width], wrecv.at[x_me], on_column(k))
+
+    exchange(3, weight_terms)
     drain(rsem, 12, bwd_p.at[partners])
     put(13, bwd_p, bwd_c, sibling)
 

time: 65.9 us -> 65.5 us (level)
  no operation moved by 1% of the time
where the time goes in v6:
time: 65.5 us; the launch traced here: 65.4 us
  Pallas kernels  64.8 us (99%)
    pallas_call x1, Pallas kernels, body(): pl.pallas_call(functools.partial(kernel_body, dims), out_shape=(results[0...  63.2 us
    pallas_call x1, Pallas kernels, body(): pl.pallas_call(deliver, out_shape=results, in_specs=[near] * 7, out_specs...  1.58 us

profile of v6, /device:TPU:1, one launch (start us, length us, event | category | flops | bytes accessed | tf_op | source)
XLA Modules:
  0.0 65.4 jit_solution(14217350704012219018)
XLA Ops:
  0.6 63.2 %operator_step.1 = (bf16[2048,256]{1,0:T(8,128)(2,1)S(1)}, f32[2048,256]{1,0:T(8,128)S(1)}, bf16[8,256,256]{2,1,0:T(8,128)(2,1)S(1)}, bf16[256,256]{1,0:T(8,128)...) custom-call(bf16[2048,256]{1,0:T(8,128)(2,1)} %bitcast.12, ...), custom_call_target="tpu_custom_call" | custom-call | tf_op jit(solution)/shard_map/operator_step/pallas_call | solution.py:453
  63.8 1.6 %deliver.1 = (bf16[2048,256]{1,0:T(8,128)(2,1)}, bf16[2048,256]{1,0:T(8,128)(2,1)}, f32[256,256]{1,0:T(8,128)}, f32[256,256]{1,0:T(8,128)}) custom-call(bf16[2048,256]{1,0:T(8,128)(2,1)S(1)} %get-tuple-element.15.y_ref, f32[2048,256]{1,0:T(8,128)S(1)} %get-tuple-element.16.local_ref, bf16[8,256,256]{2,1,0:T(8,128)(2,1)S(1)} %get-tuple-element.17.tab_ref, ...), custom_call_target="tpu_custom_call" | custom-call | tf_op jit(solution)/shard_map/deliver/pallas_call | solution.py:495
